TPU v7x, 32 devices: a whole 2x2x4 slice. The times are simulated.
32 devices in a mesh: rep: 4 (over y, x), seq: 8 (over z, core).
Axes of the slice: x: 2, y: 2, z: 4, core: 2. Of those that a mesh axis runs over, the one named last changes fastest.
Arguments:
- query: bfloat16 [4096, 2048], P(('rep', 'seq')), parts along dimension 0, may hold values from -6 to 6
- key_proj: bfloat16 [4096, 2048], P(('rep', 'seq')), parts along dimension 0, may hold values from -6 to 6
- value: bfloat16 [4096, 2048], P(('rep', 'seq')), parts along dimension 0, may hold values from -6 to 6
- poles: float32 [2048, 16], replicated, may hold values from 0.00048828125 to 0.05
- residues: float32 [2048, 16], replicated, may hold values from -0.12 to 0.12
- skip: float32 [2048], replicated, may hold values from 0.5 to 2
- w_out: bfloat16 [2048, 4096], P('seq'), may hold values from -0.125 to 0.125
Outputs:
- mixed: bfloat16 [4096, 4096], P(('rep', 'seq')), parts along dimension 0
There are 4 independent parts, one for each index of `rep`. A program takes and returns all parts, laid end to end along the dimension named above; an argument that names none is the same for every part. Nothing has to cross between parts.
All inputs are finite; a program needn't handle non-finite values.
Results may differ from a plain program's by a relative error of at most 0.012.
Values may be sent and summed in bfloat16 or wider, within the bound.
No kernel may reach another device: no remote copies, remote signals or barrier semaphores. Data moves between devices by JAX's collectives and lax.ppermute only.
A program may use at most 128 MiB of HBM per device.

v0:
```python
import functools
import math

import jax
import jax.numpy as jnp
from jax import lax
from jax.experimental import pallas as pl
from jax.experimental.pallas import tpu as pltpu
from jax.sharding import PartitionSpec as P


F32 = jnp.float32
BF16 = jnp.bfloat16
LANES = 128
SUBLANES = 8


def permute(array, axis, target):
    size = lax.axis_size(axis)
    return lax.ppermute(array, axis, [(i, target(i)) for i in range(size)])


def swap(array, axis, mask):
    return permute(array, axis, lambda i: i ^ mask)


def fill_product(key_ref, value_ref, prod_ref):
    tokens, channels = key_ref.shape
    for tile in range(channels // LANES):
        cols = slice(tile * LANES, (tile + 1) * LANES)
        prod_ref[tile * tokens : (tile + 1) * tokens, :] = key_ref[:, cols].astype(F32) * value_ref[:, cols].astype(F32)


def group_of(core_ref, slot, tiles):
    half = tiles // 2
    side = core_ref[0] if slot == 0 else 1 - core_ref[0]
    return pl.multiple_of(side * half, SUBLANES), half


def state_kernel(core_ref, key_ref, value_ref, poles_ref, kept_ref, sent_ref, rate_ref, prod_ref):
    tokens = key_ref.shape[0]
    order, tiles, _ = poles_ref.shape
    fill_product(key_ref, value_ref, prod_ref)
    for slot, state_ref in ((1, sent_ref), (0, kept_ref)):
        start, half = group_of(core_ref, slot, tiles)
        for row in range(0, half, SUBLANES):
            first = pl.multiple_of(start + row, SUBLANES)
            poles = [poles_ref[r, pl.ds(first, SUBLANES), :] for r in range(order)]
            decay = [jnp.exp(-p) for p in poles]

            def step(t, state):
                x = prod_ref[pl.ds(first * tokens + t, SUBLANES, stride=tokens), :]
                return tuple(decay[r] * state[r] + x for r in range(order))

            zero = jnp.zeros((SUBLANES, LANES), F32)
            state = lax.fori_loop(0, tokens, step, (zero,) * order, unroll=8)
            for r in range(order):
                state_ref[r, row : row + SUBLANES, :] = state[r]
                if slot == 0:
                    rate_ref[r, row : row + SUBLANES, :] = jnp.exp(-poles[r] * float(tokens))


def local_kernel(key_ref, value_ref, poles_ref, residues_ref, skip_ref, local_ref):
    tokens = key_ref.shape[0]
    order, tiles, _ = poles_ref.shape
    fill_product(key_ref, value_ref, local_ref)
    for first in range(0, tiles, SUBLANES):
        group = slice(first, first + SUBLANES)
        decay = [jnp.exp(-poles_ref[r, group, :]) for r in range(order)]
        skip = skip_ref[group, :]

        def step(t, state):
            rows = pl.ds(first * tokens + t, SUBLANES, stride=tokens)
            x = local_ref[rows, :]
            state = tuple(decay[r] * state[r] + x for r in range(order))
            parts = [residues_ref[r, group, :] * state[r] for r in range(order)] + [skip * x]
            local_ref[rows, :] = tree_sum(parts)
            return state

        zero = jnp.zeros((SUBLANES, LANES), F32)
        lax.fori_loop(0, tokens, step, (zero,) * order, unroll=4)


def tree_sum(parts):
    while len(parts) > 1:
        parts = [parts[i] if i + 1 == len(parts) else parts[i] + parts[i + 1] for i in range(0, len(parts), 2)]
    return parts[0]


def carry_kernel(core_ref, query_ref, local_ref, poles_ref, residues_ref, kept_ref, sent_ref, *refs):
    gated_refs, total_ref, starts_ref = refs[:-2], refs[-2], refs[-1]
    tokens, channels = query_ref.shape
    order, tiles, _ = poles_ref.shape
    stretch = 16 if tokens % 16 == 0 else tokens
    for slot, carry_ref in ((0, kept_ref), (1, sent_ref)):
        start, half = group_of(core_ref, slot, tiles)
        for row in range(0, half, SUBLANES):
            first = pl.multiple_of(start + row, SUBLANES)
            group = pl.ds(first, SUBLANES)
            jump = [jnp.exp(-poles_ref[r, group, :] * float(stretch)) for r in range(order)]
            state = [carry_ref[r, row : row + SUBLANES, :] for r in range(order)]
            for i in range(tokens // stretch):
                for r in range(order):
                    starts_ref[i, r] = state[r]
                state = [jump[r] * state[r] for r in range(order)]
            decay = [jnp.exp(-poles_ref[r, group, :]) for r in range(order)]

            def step(j, weight):
                weight = tuple(decay[r] * weight[r] for r in range(order))
                for i in range(tokens // stretch):
                    rows = pl.ds(first * tokens + i * stretch + j, SUBLANES, stride=tokens)
                    parts = [weight[r] * starts_ref[i, r] for r in range(order)] + [local_ref[rows, :]]
                    total_ref[rows, :] = tree_sum(parts)
                return weight

            lax.fori_loop(0, stretch, step, tuple(residues_ref[r, group, :] for r in range(order)))
    step_rows = tokens // len(gated_refs)
    for tile in range(channels // LANES):
        cols = slice(tile * LANES, (tile + 1) * LANES)
        y = total_ref[tile * tokens : (tile + 1) * tokens, :]
        gated = (query_ref[:, cols].astype(F32) * y).astype(BF16)
        for i, ref in enumerate(gated_refs):
            ref[:, cols] = gated[i * step_rows : (i + 1) * step_rows, :]


def project_kernel(pieces, blocks, chunks, index_ref, *refs):
    gated, weights = refs[:pieces], [refs[pieces + n * blocks : pieces + (n + 1) * blocks] for n in range(chunks)]
    outs, (left, right, left_sem, right_sem) = refs[pieces + chunks * blocks : -4], refs[-4:]
    tokens = gated[0].shape[0]
    depth, columns = weights[0][0].shape
    copies = []
    for n in range(chunks):
        for b in range(blocks):
            start = pl.multiple_of(index_ref[b] * depth, depth)
            place = right.at[pl.ds(start, depth), pl.ds(n * columns, columns)]
            copies.append(pltpu.make_async_copy(weights[n][b], place, right_sem.at[n * blocks + b]))
    for i in range(pieces):
        copies.append(pltpu.make_async_copy(gated[i], left.at[pl.ds(i * tokens, tokens), :], left_sem.at[i]))
    for copy in copies:
        copy.start()
    for copy in copies:
        copy.wait()
    total = jnp.dot(left[...], right[...], preferred_element_type=F32).astype(BF16)
    rows = total.shape[0] // len(outs)
    for i, out in enumerate(outs):
        out[...] = total[i * rows : (i + 1) * rows, :]


def place_kernel(aliased, index_ref, *refs):
    pieces, (out_ref, held, in_sem, out_sem) = refs[:-4], refs[-4:]
    if aliased:
        pieces = pieces[1:]
    arrive = [pltpu.make_async_copy(piece, held.at[i], in_sem.at[i]) for i, piece in enumerate(pieces)]
    for copy in arrive:
        copy.start()
    leave = []
    for i, piece in enumerate(pieces):
        width = piece.shape[1]
        start = pl.multiple_of(index_ref[i] * width, width)
        leave.append(pltpu.make_async_copy(held.at[i], out_ref.at[:, pl.ds(start, width)], out_sem.at[i]))
    for i in range(len(pieces)):
        arrive[i].wait()
        leave[i].start()
    for copy in leave:
        copy.wait()


def whole(count, space=pltpu.VMEM):
    return [pl.BlockSpec(memory_space=space)] * count


def call(kernel, out_shapes, args, scratch=(), scalars=0, flops=0, inputs=pltpu.VMEM, outputs=pltpu.VMEM, aliases=None):
    out_shapes = [jax.ShapeDtypeStruct(s, d) for s, d in out_shapes]
    moved = sum(a.size * a.dtype.itemsize for a in list(args) + out_shapes)
    held = sum(math.prod(m.shape) * jnp.dtype(m.dtype).itemsize for m in scratch if m.memory_space == pltpu.VMEM)
    held += moved if inputs == pltpu.VMEM else 0
    return pl.pallas_call(
        kernel,
        out_shape=out_shapes,
        in_specs=whole(scalars, pltpu.SMEM) + whole(len(args) - scalars, inputs),
        out_specs=whole(len(out_shapes), outputs),
        scratch_shapes=list(scratch),
        input_output_aliases=aliases or {},
        compiler_params=pltpu.CompilerParams(vmem_limit_bytes=min(2 * held + (4 << 20), 60 << 20)),
        cost_estimate=pl.CostEstimate(flops=flops, bytes_accessed=moved, transcendentals=0),
    )(*args)


def carry_in(kept, sent, rate, members):
    seq = lax.axis_index("seq")
    first = seq % 2 == 0
    other = swap(sent, "seq", 1)
    early = jnp.where(first, kept, other)
    total = rate * early + jnp.where(first, other, kept)
    prefix = jnp.zeros_like(total)
    ahead = jnp.ones_like(total)
    step = rate * rate
    span = 2
    while span < members:
        arrived = swap(total, "seq", span)
        upper = (seq // span) % 2 == 1
        prefix = prefix + jnp.where(upper, ahead * arrived, 0.0)
        ahead = jnp.where(upper, ahead * step, ahead)
        total = step * jnp.where(upper, arrived, total) + jnp.where(upper, total, arrived)
        step = step * step
        span *= 2
    later = rate * prefix + early
    rest = swap(jnp.where(first, later, prefix), "seq", 1)
    return jnp.where(first, prefix, later), rest


def gather_rows(block, members):
    seq = lax.axis_index("seq")
    if members != 8:
        rows = lax.all_gather(block, "seq", axis=0, tiled=True)
        return [rows], jnp.zeros((1,), jnp.int32)
    spot = seq // 2
    inner = (spot == 1) | (spot == 2)

    def middle(i):
        return {2: 4, 3: 5, 4: 2, 5: 3}.get(i, i ^ 1)

    near = swap(block, "seq", 2)
    across = permute(block, "seq", middle)
    near_next = swap(across, "seq", 2)
    across_next = permute(near, "seq", middle)
    far = swap(across_next, "seq", 2)
    second = jnp.where(inner, across, near_next)
    third = jnp.where(inner, across_next, far)
    mine = [block, near, second, third]
    theirs = [swap(b, "seq", 1) for b in mine]
    core = seq % 2
    spots = [spot, spot ^ 1, jnp.where(inner, 3 - spot, spot ^ 2), jnp.where(inner, spot ^ 2, 3 - spot)]
    places = [p * 2 + core for p in spots] + [p * 2 + 1 - core for p in spots]
    return mine + theirs, jnp.stack(places).astype(jnp.int32)


def gather_parts(halves, parts):
    if parts != 4 or len(halves) != 2:
        return [halves] + [[swap(h, "rep", i) for h in halves] for i in range(1, parts)]
    one = [swap(h, "rep", 1) for h in halves]
    two = [swap(h, "rep", 2) for h in halves]
    three = [swap(two[0], "rep", 1), swap(one[1], "rep", 2)]
    return [halves, one, two, three]


def shards(chunks, query, key_proj, value, poles, residues, skip, w_out):
    tokens, channels = query.shape
    width = w_out.shape[1]
    members = lax.axis_size("seq")
    parts = lax.axis_size("rep")
    order = poles.shape[1]
    tiles = channels // LANES
    rep = lax.axis_index("rep")
    part_width = width // parts
    columns = part_width // chunks

    weights = []
    for n in range(chunks):
        block = lax.dynamic_slice_in_dim(w_out, (rep * chunks + n) * columns, columns, 1)
        rows, places = gather_rows(block, members)
        weights.append(rows)

    poles = poles.T.reshape(order, tiles, LANES)
    residues = residues.T.reshape(order, tiles, LANES)
    skip = skip.reshape(tiles, LANES)
    core = (lax.axis_index("seq") % 2).astype(jnp.int32).reshape(1)
    sums = pltpu.VMEM((tiles * tokens, LANES), F32)
    work = tokens * channels * order
    state_shape = ((order, tiles // 2, LANES), F32)
    kept, sent, rate = call(
        state_kernel, [state_shape] * 3, (core, key_proj, value, poles), [sums], scalars=1, flops=2 * work
    )
    kept, sent = carry_in(kept, sent, rate, members)
    (local,) = call(
        local_kernel, [((tiles * tokens, LANES), F32)], (key_proj, value, poles, residues, skip), flops=4 * work
    )
    halves = call(
        carry_kernel,
        [((tokens // 2, channels), BF16)] * 2,
        (core, query, local, poles, residues, kept, sent),
        [sums, pltpu.VMEM((tokens // 16, order, SUBLANES, LANES), F32)],
        scalars=1,
        flops=2 * work,
    )
    gathered = gather_parts(list(halves), parts)
    count = len(weights[0])
    blocks = []
    for group in (gathered[:-1], gathered[-1:]):
        held = sum(group, [])
        blocks += call(
            functools.partial(project_kernel, len(held), count, chunks),
            [((tokens, part_width), BF16)] * len(group),
            (places, *held, *sum(weights, [])),
            [
                pltpu.VMEM((len(group) * tokens, channels), BF16),
                pltpu.VMEM((channels, part_width), BF16),
                pltpu.SemaphoreType.DMA((len(held),)),
                pltpu.SemaphoreType.DMA((chunks * count,)),
            ],
            scalars=1,
            flops=2 * len(group) * tokens * channels * part_width,
            inputs=pl.ANY,
        )
    pieces = [blocks[0]] + [swap(blocks[i], "rep", i) for i in range(1, parts)]
    spots = (rep ^ jnp.arange(parts, dtype=jnp.int32)).astype(jnp.int32)
    mixed = None
    for group in (range(parts - 1), range(parts - 1, parts)):
        first = mixed is None
        (mixed,) = call(
            functools.partial(place_kernel, not first),
            [((tokens, width), BF16)],
            (spots[group[0] :], *([] if first else [mixed]), *[pieces[i] for i in group]),
            [
                pltpu.VMEM((len(group), tokens, part_width), BF16),
                pltpu.SemaphoreType.DMA((len(group),)),
                pltpu.SemaphoreType.DMA((len(group),)),
            ],
            scalars=1,
            inputs=pl.ANY,
            outputs=pl.ANY,
            aliases=None if first else {1: 0},
        )
    return mixed


def solution(mesh):
    chunks = 2

    def body(*args):
        return shards(chunks, *args)

    return jax.shard_map(
        body,
        mesh=mesh,
        in_specs=(
            P(("rep", "seq"), None),
            P(("rep", "seq"), None),
            P(("rep", "seq"), None),
            P(),
            P(),
            P(),
            P("seq", None),
        ),
        out_specs=P(("rep", "seq"), None),
        check_vma=False,
    )
```

profile of v0, /device:TPU:0, one launch (start us, length us, event | category | flops | bytes accessed | tf_op | source)
XLA Modules:
  0.0 87.2 jit_solution(6260880917737947388)
XLA Ops:
  1.0 1.0 %copy-done = bf16[128,2048]{1,0:T(8,128)(2,1)S(1)} copy-done((bf16[128,2048]{1,0:T(8,128)(2,1)S(1)}, bf16[128,2048]{1,0:T(8,128)(2,1)}, u32[]{:S(2)}) %copy-start) | copy-done | bytes 524312
  2.0 1.0 %copy-done.2 = bf16[128,2048]{1,0:T(8,128)(2,1)S(1)} copy-done((bf16[128,2048]{1,0:T(8,128)(2,1)S(1)}, bf16[128,2048]{1,0:T(8,128)(2,1)}, u32[]{:S(2)}) %copy-start.2) | copy-done | bytes 524312
  3.0 1.7 %shard_map.74 = (f32[16,8,128]{2,1,0:T(8,128)S(1)}, f32[16,8,128]{2,1,0:T(8,128)S(1)}, f32[16,8,128]{2,1,0:T(8,128)S(1)}) custom-call(s32[1]{0:T(128)} %bitcast.8.core_ref, bf16[128,2048]{1,0:T(8,128)(2,1)S(1)} %copy-done, bf16[128,2048]{1,0:T(8,128)(2,1)S(1)} %copy-done.2, f32[16,16,128]{2,1,0:T(8,128)S(1)} %bitcast.16), custom_call_target="tpu_custom_call" | custom-call | flops 8388608 | bytes 1376260 | tf_op jit(solution)/shard_map/pallas_call | solution.py:177
  6.2 3.0 %collective-permute-start.1 = (f32[16,8,128]{2,1,0:T(8,128)S(1)}, f32[16,8,128]{2,1,0:T(8,128)S(1)}, u32[]{:S(2)}, u32[]{:S(2)}) collective-permute-start(f32[16,8,128]{2,1,0:T(8,128)S(1)} %select_add_fusion.2), channel_id=1, source_target_pairs={{0,2},{1,3},{2,0},{3,1},{4,6},{5,7},{6,4},{7,5},{8,10},{9,11},{10,... | collective-permute-start | bytes 196616 | tf_op jit(solution)/shard_map/ppermute | solution.py:20
  9.2 2.4 %collective-permute-done.1 = f32[16,8,128]{2,1,0:T(8,128)S(1)} collective-permute-done((f32[16,8,128]{2,1,0:T(8,128)S(1)}, f32[16,8,128]{2,1,0:T(8,128)S(1)}, u32[]{:S(2)}, u32[]{:S(2)}) %collective-permute-start.1) | collective-permute-done | bytes 65568 | tf_op jit(solution)/shard_map/ppermute | solution.py:20
  11.7 2.9 %collective-permute-start.2 = (f32[16,8,128]{2,1,0:T(8,128)S(1)}, f32[16,8,128]{2,1,0:T(8,128)S(1)}, u32[]{:S(2)}, u32[]{:S(2)}) collective-permute-start(f32[16,8,128]{2,1,0:T(8,128)S(1)} %select_add_fusion.1), channel_id=1, source_target_pairs={{0,4},{1,5},{2,6},{3,7},{4,0},{5,1},{6,2},{7,3},{8,12},{9,13},{10,... | collective-permute-start | bytes 196616 | tf_op jit(solution)/shard_map/ppermute | solution.py:20
  14.6 1.1 %constant_dynamic-slice_fusion = (bf16[256,512]{1,0:T(8,128)(2,1)S(1)}, bf16[256,512]{1,0:T(8,128)(2,1)S(1)}) fusion(bf16[256,4096]{1,0:T(8,128)(2,1)} %param.13, s32[]{:T(128)S(6)} %select_n.129, s32[]{:T(128)S(6)} %select_n.125), kind=kLoop, calls=%fused_computation.11 | loop fusion | bytes 1048584 | tf_op jit(solution)/shard_map/dynamic_slice | solution.py:260
  15.7 1.6 %collective-permute-start.8 = (bf16[256,512]{1,0:T(8,128)(2,1)S(1)}, bf16[256,512]{1,0:T(8,128)(2,1)S(1)}, u32[]{:S(2)}, u32[]{:S(2)}) collective-permute-start(bf16[256,512]{1,0:T(8,128)(2,1)S(1)} %get-tuple-element.22.refs_6_.refs_2_), channel_id=1, source_target_pairs={{0,2},{1,3},{2,0},{3,1},{4,6},{5,7},{6,4},{7,5},{8,10},{9,11},{10,... | collective-permute-start | bytes 786440 | tf_op jit(solution)/shard_map/ppermute | solution.py:20
  18.0 2.7 %collective-permute-start.17 = (bf16[256,512]{1,0:T(8,128)(2,1)S(1)}, bf16[256,512]{1,0:T(8,128)(2,1)S(1)}, u32[]{:S(2)}, u32[]{:S(2)}) collective-permute-start(bf16[256,512]{1,0:T(8,128)(2,1)S(1)} %get-tuple-element.21.refs_14_.refs_10_), channel_id=1, source_target_pairs={{0,2},{1,3},{2,0},{3,1},{4,6},{5,7},{6,4},{7,5},{8,10},{9,11},{10,... | collective-permute-start | bytes 786440 | tf_op jit(solution)/shard_map/ppermute | solution.py:20
  20.7 6.1 %collective-permute-start.10 = (bf16[256,512]{1,0:T(8,128)(2,1)S(1)}, bf16[256,512]{1,0:T(8,128)(2,1)}, u32[]{:S(2)}, u32[]{:S(2)}) collective-permute-start(bf16[256,512]{1,0:T(8,128)(2,1)S(1)} %collective-permute-done.9), channel_id=1, source_target_pairs={{0,2},{1,3},{2,0},{3,1},{4,6},{5,7},{6,4},{7,5},{8,10},{9,11},{10,... | collective-permute-start | bytes 786440 | tf_op jit(solution)/shard_map/ppermute | solution.py:20
  26.8 5.7 %collective-permute-start.19 = (bf16[256,512]{1,0:T(8,128)(2,1)}, bf16[256,512]{1,0:T(8,128)(2,1)}, u32[]{:S(2)}, u32[]{:S(2)}) collective-permute-start(bf16[256,512]{1,0:T(8,128)(2,1)} %collective-permute-done.18), channel_id=1, source_target_pairs={{0,2},{1,3},{2,0},{3,1},{4,6},{5,7},{6,4},{7,5},{8,10},{9,11},{10,... | collective-permute-start | bytes 786440 | tf_op jit(solution)/shard_map/ppermute | solution.py:20
  33.5 3.8 %shard_map.73.local_ref = f32[2048,128]{1,0:T(8,128)S(1)} custom-call(bf16[128,2048]{1,0:T(8,128)(2,1)S(1)} %copy-done.1, bf16[128,2048]{1,0:T(8,128)(2,1)S(1)} %copy-done.3, f32[16,16,128]{2,1,0:T(8,128)S(1)} %bitcast.17, f32[16,16,128]{2,1,0:T(8,128)S(1)} %bitcast.19, f32[16,128]{1,0:T(8,128)S(1)} %bitcast.21), custom_call_target="tpu_custom_call" | custom-call | flops 16777216 | bytes 2367488 | tf_op jit(solution)/shard_map/pallas_call | solution.py:177
  37.3 2.4 %shard_map.75 = (bf16[64,2048]{1,0:T(8,128)(2,1)S(1)}, bf16[64,2048]{1,0:T(8,128)(2,1)S(1)}) custom-call(s32[1]{0:T(128)} %bitcast.8.core_ref, bf16[128,2048]{1,0:T(8,128)(2,1)S(1)} %copy-done.4, f32[2048,128]{1,0:T(8,128)S(1)} %shard_map.73.local_ref, f32[16,16,128]{2,1,0:T(8,128)S(1)} %bitcast.18, f32[16,16,128]{2,1,0:T(8,128)S(1)} %bitcast.20, ...), custom_call_target="tpu_custom_call" | custom-call | flops 8388608 | bytes 2490372 | tf_op jit(solution)/shard_map/pallas_call | solution.py:177
  40.3 1.5 %collective-permute-start.4 = (bf16[64,2048]{1,0:T(8,128)(2,1)S(1)}, bf16[64,2048]{1,0:T(8,128)(2,1)S(1)}, u32[]{:S(2)}, u32[]{:S(2)}) collective-permute-start(bf16[64,2048]{1,0:T(8,128)(2,1)S(1)} %get-tuple-element.16.refs_0_), channel_id=1, source_target_pairs={{0,8},{8,0},{16,24},{24,16},{1,9},{9,1},{17,25},{25,17},{2,10},{10... | collective-permute-start | bytes 786440 | tf_op jit(solution)/shard_map/ppermute | solution.py:20
  42.0 1.0 %broadcast_select_fusion.3.refs_8_.refs_4_ = bf16[256,512]{1,0:T(8,128)(2,1)S(1)} fusion(bf16[256,512]{1,0:T(8,128)(2,1)S(1)} %collective-permute-done.9, bf16[256,512]{1,0:T(8,128)(2,1)} %collective-permute-done.10, pred[]{:T(512)S(6)} %or.4), kind=kLoop, calls=%fused_computation.3 | loop fusion | flops 131072 | bytes 786433 | tf_op jit(solution)/shard_map/jit(_where)/select_n | solution.py:228
  44.5 1.0 %broadcast_select_fusion.1.refs_16_.refs_12_ = bf16[256,512]{1,0:T(8,128)(2,1)S(1)} fusion(bf16[256,512]{1,0:T(8,128)(2,1)} %collective-permute-done.18, bf16[256,512]{1,0:T(8,128)(2,1)} %collective-permute-done.19, pred[]{:T(512)S(6)} %or.4), kind=kLoop, calls=%fused_computation.1 | loop fusion | flops 131072 | bytes 786433 | tf_op jit(solution)/shard_map/jit(_where)/select_n | solution.py:228
  45.5 1.6 %collective-permute-start.6 = (bf16[64,2048]{1,0:T(8,128)(2,1)S(1)}, bf16[64,2048]{1,0:T(8,128)(2,1)}, u32[]{:S(2)}, u32[]{:S(2)}) collective-permute-start(bf16[64,2048]{1,0:T(8,128)(2,1)S(1)} %get-tuple-element.16.refs_0_), channel_id=1, source_target_pairs={{0,16},{8,24},{16,0},{24,8},{1,17},{9,25},{17,1},{25,9},{2,18},{10... | collective-permute-start | bytes 786440 | tf_op jit(solution)/shard_map/ppermute | solution.py:20
  47.1 2.4 %collective-permute-done.4.refs_2_ = bf16[64,2048]{1,0:T(8,128)(2,1)S(1)} collective-permute-done((bf16[64,2048]{1,0:T(8,128)(2,1)S(1)}, bf16[64,2048]{1,0:T(8,128)(2,1)S(1)}, u32[]{:S(2)}, u32[]{:S(2)}) %collective-permute-start.4) | collective-permute-done | bytes 262176 | tf_op jit(solution)/shard_map/ppermute | solution.py:20
  50.2 1.5 %collective-permute-start.7 = (bf16[64,2048]{1,0:T(8,128)(2,1)S(1)}, bf16[64,2048]{1,0:T(8,128)(2,1)S(1)}, u32[]{:S(2)}, u32[]{:S(2)}) collective-permute-start(bf16[64,2048]{1,0:T(8,128)(2,1)S(1)} %get-tuple-element.17.refs_1_), channel_id=1, source_target_pairs={{0,16},{8,24},{16,0},{24,8},{1,17},{9,25},{17,1},{25,9},{2,18},{10... | collective-permute-start | bytes 786440 | tf_op jit(solution)/shard_map/ppermute | solution.py:20
  51.8 2.6 %collective-permute-done.5.refs_3_ = bf16[64,2048]{1,0:T(8,128)(2,1)} collective-permute-done((bf16[64,2048]{1,0:T(8,128)(2,1)S(1)}, bf16[64,2048]{1,0:T(8,128)(2,1)}, u32[]{:S(2)}, u32[]{:S(2)}) %collective-permute-start.5) | collective-permute-done | bytes 262176 | tf_op jit(solution)/shard_map/ppermute | solution.py:20
  54.3 1.3 %collective-permute-done.21 = bf16[256,512]{1,0:T(8,128)(2,1)S(1)} collective-permute-done((bf16[256,512]{1,0:T(8,128)(2,1)}, bf16[256,512]{1,0:T(8,128)(2,1)S(1)}, u32[]{:S(2)}, u32[]{:S(2)}) %collective-permute-start.21) | collective-permute-done | bytes 262176 | tf_op jit(solution)/shard_map/ppermute | solution.py:20
  56.3 2.1 %collective-permute-done.7.refs_5_ = bf16[64,2048]{1,0:T(8,128)(2,1)S(1)} collective-permute-done((bf16[64,2048]{1,0:T(8,128)(2,1)S(1)}, bf16[64,2048]{1,0:T(8,128)(2,1)S(1)}, u32[]{:S(2)}, u32[]{:S(2)}) %collective-permute-start.7) | collective-permute-done | bytes 262176 | tf_op jit(solution)/shard_map/ppermute | solution.py:20
  59.5 1.5 %collective-permute-start.28 = (bf16[64,2048]{1,0:T(8,128)(2,1)}, bf16[64,2048]{1,0:T(8,128)(2,1)}, u32[]{:S(2)}, u32[]{:S(2)}) collective-permute-start(bf16[64,2048]{1,0:T(8,128)(2,1)} %collective-permute-done.6.refs_4_), channel_id=1, source_target_pairs={{0,8},{8,0},{16,24},{24,16},{1,9},{9,1},{17,25},{25,17},{2,10},{10... | collective-permute-start | bytes 786440 | tf_op jit(solution)/shard_map/ppermute | solution.py:20
  61.0 1.6 %collective-permute-start.29 = (bf16[64,2048]{1,0:T(8,128)(2,1)}, bf16[64,2048]{1,0:T(8,128)(2,1)}, u32[]{:S(2)}, u32[]{:S(2)}) collective-permute-start(bf16[64,2048]{1,0:T(8,128)(2,1)} %collective-permute-done.5.refs_3_), channel_id=1, source_target_pairs={{0,16},{8,24},{16,0},{24,8},{1,17},{9,25},{17,1},{25,9},{2,18},{10... | collective-permute-start | bytes 786440 | tf_op jit(solution)/shard_map/ppermute | solution.py:20
  63.7 0.9 %copy-done.9 = bf16[64,2048]{1,0:T(8,128)(2,1)S(1)} copy-done((bf16[64,2048]{1,0:T(8,128)(2,1)S(1)}, bf16[64,2048]{1,0:T(8,128)(2,1)}, u32[]{:S(2)}) %copy-start.9) | copy-done | bytes 262168
  66.5 4.0 %shard_map.76 = (bf16[128,1024]{1,0:T(8,128)(2,1)S(1)}, bf16[128,1024]{1,0:T(8,128)(2,1)S(1)}, bf16[128,1024]{1,0:T(8,128)(2,1)S(1)}) custom-call(s32[8]{0:T(128)S(1)} %stack.35.index_ref, bf16[64,2048]{1,0:T(8,128)(2,1)S(1)} %copy-done.7, bf16[64,2048]{1,0:T(8,128)(2,1)S(1)} %copy-done.9, bf16[64,2048]{1,0:T(8,128)(2,1)S(1)} %copy-done.11, ...), custom_call_target="tpu_custom_call" | custom-call | flops 1610612736 | bytes 6553632 | tf_op jit(solution)/shard_map/pallas_call | solution.py:177
  72.0 2.9 %shard_map.78 = bf16[128,1024]{1,0:T(8,128)(2,1)S(1)} custom-call(s32[8]{0:T(128)S(1)} %stack.35.index_ref, bf16[64,2048]{1,0:T(8,128)(2,1)} %collective-permute-done.28.refs_0_, bf16[64,2048]{1,0:T(8,128)(2,1)} %collective-permute-done.29.refs_1_, bf16[256,512]{1,0:T(8,128)(2,1)S(1)} %get-tuple-element.22.refs_6_.refs_2_, ...), custom_call_target="tpu_custom_call" | custom-call | flops 536870912 | bytes 4980768 | tf_op jit(solution)/shard_map/pallas_call | solution.py:177
  74.9 2.2 %collective-permute-start.30 = (bf16[128,1024]{1,0:T(8,128)(2,1)S(1)}, bf16[128,1024]{1,0:T(8,128)(2,1)S(1)}, u32[]{:S(2)}, u32[]{:S(2)}) collective-permute-start(bf16[128,1024]{1,0:T(8,128)(2,1)S(1)} %shard_map.78), channel_id=1, source_target_pairs={{0,24},{8,16},{16,8},{24,0},{1,25},{9,17},{17,9},{25,1},{2,26},{10... | collective-permute-start | bytes 786440 | tf_op jit(solution)/shard_map/ppermute | solution.py:20
  77.7 1.8 %collective-permute-done.26.refs_1_ = bf16[128,1024]{1,0:T(8,128)(2,1)S(1)} collective-permute-done((bf16[128,1024]{1,0:T(8,128)(2,1)S(1)}, bf16[128,1024]{1,0:T(8,128)(2,1)S(1)}, u32[]{:S(2)}, u32[]{:S(2)}) %collective-permute-start.26) | collective-permute-done | bytes 262176 | tf_op jit(solution)/shard_map/ppermute | solution.py:20
  79.5 4.7 %collective-permute-done.27.refs_2_ = bf16[128,1024]{1,0:T(8,128)(2,1)S(1)} collective-permute-done((bf16[128,1024]{1,0:T(8,128)(2,1)S(1)}, bf16[128,1024]{1,0:T(8,128)(2,1)S(1)}, u32[]{:S(2)}, u32[]{:S(2)}) %collective-permute-start.27) | collective-permute-done | bytes 262176 | tf_op jit(solution)/shard_map/ppermute | solution.py:20
  84.2 1.5 %shard_map.77.refs_0_ = bf16[128,4096]{1,0:T(8,128)(2,1)} custom-call(s32[4]{0:T(128)S(1)} %iota_xor_fusion.index_ref, bf16[128,1024]{1,0:T(8,128)(2,1)S(1)} %get-tuple-element.18.refs_0_, bf16[128,1024]{1,0:T(8,128)(2,1)S(1)} %collective-permute-done.26.refs_1_, bf16[128,1024]{1,0:T(8,128)(2,1)S(1)} %collective-permute-done.27.refs_2_), custom_call_target="tpu_custom_call" | custom-call | bytes 1835024 | tf_op jit(solution)/shard_map/pallas_call | solution.py:177
  85.8 1.4 %shard_map.79 = bf16[128,4096]{1,0:T(8,128)(2,1)} custom-call(s32[1]{0:T(128)} %slice.3.index_ref, bf16[128,4096]{1,0:T(8,128)(2,1)} %shard_map.77.refs_0_, bf16[128,1024]{1,0:T(8,128)(2,1)S(1)} %collective-permute-done.30.refs_1_), custom_call_target="tpu_custom_call", output_to_operand_aliasing={{}: (1, {})} | custom-call | bytes 2359300 | tf_op jit(solution)/shard_map/pallas_call | solution.py:177
  (78 shorter events, 14.0 us)
Async XLA Ops:
  0.0 33.5 %copy-start.5 = (f32[2048]{0:T(1024)S(1)}, f32[2048]{0:T(1024)}, u32[]{:S(2)}) copy-start(f32[2048]{0:T(1024)} %param.12) | copy-start | bytes 24580
  4.8 1.5 %collective-permute-start = (f32[16,8,128]{2,1,0:T(8,128)S(1)}, f32[16,8,128]{2,1,0:T(8,128)S(1)}, u32[]{:S(2)}, u32[]{:S(2)}) collective-permute-start(f32[16,8,128]{2,1,0:T(8,128)S(1)} %get-tuple-element.15), channel_id=1, source_target_pairs={{0,1},{1,0},{2,3},{3,2},{4,5},{5,4},{6,7},{7,6},{8,9},{9,8},{10,11... | collective-permute-start | bytes 196616 | tf_op jit(solution)/shard_map/ppermute | solution.py:20
  6.2 5.4 %collective-permute-start.1 = (f32[16,8,128]{2,1,0:T(8,128)S(1)}, f32[16,8,128]{2,1,0:T(8,128)S(1)}, u32[]{:S(2)}, u32[]{:S(2)}) collective-permute-start(f32[16,8,128]{2,1,0:T(8,128)S(1)} %select_add_fusion.2), channel_id=1, source_target_pairs={{0,2},{1,3},{2,0},{3,1},{4,6},{5,7},{6,4},{7,5},{8,10},{9,11},{10,... | collective-permute-start | bytes 196616 | tf_op jit(solution)/shard_map/ppermute | solution.py:20
  11.7 5.6 %collective-permute-start.2 = (f32[16,8,128]{2,1,0:T(8,128)S(1)}, f32[16,8,128]{2,1,0:T(8,128)S(1)}, u32[]{:S(2)}, u32[]{:S(2)}) collective-permute-start(f32[16,8,128]{2,1,0:T(8,128)S(1)} %select_add_fusion.1), channel_id=1, source_target_pairs={{0,4},{1,5},{2,6},{3,7},{4,0},{5,1},{6,2},{7,3},{8,12},{9,13},{10,... | collective-permute-start | bytes 196616 | tf_op jit(solution)/shard_map/ppermute | solution.py:20
  15.7 11.2 %collective-permute-start.8 = (bf16[256,512]{1,0:T(8,128)(2,1)S(1)}, bf16[256,512]{1,0:T(8,128)(2,1)S(1)}, u32[]{:S(2)}, u32[]{:S(2)}) collective-permute-start(bf16[256,512]{1,0:T(8,128)(2,1)S(1)} %get-tuple-element.22.refs_6_.refs_2_), channel_id=1, source_target_pairs={{0,2},{1,3},{2,0},{3,1},{4,6},{5,7},{6,4},{7,5},{8,10},{9,11},{10,... | collective-permute-start | bytes 786440 | tf_op jit(solution)/shard_map/ppermute | solution.py:20
  17.3 3.4 %collective-permute-start.9 = (bf16[256,512]{1,0:T(8,128)(2,1)S(1)}, bf16[256,512]{1,0:T(8,128)(2,1)S(1)}, u32[]{:S(2)}, u32[]{:S(2)}) collective-permute-start(bf16[256,512]{1,0:T(8,128)(2,1)S(1)} %get-tuple-element.22.refs_6_.refs_2_), channel_id=1, source_target_pairs={{0,1},{1,0},{2,4},{3,5},{4,2},{5,3},{6,7},{7,6},{8,9},{9,8},{10,12... | collective-permute-start | bytes 786440 | tf_op jit(solution)/shard_map/ppermute | solution.py:20
  17.3 3.4 %collective-permute-start.3 = (f32[16,8,128]{2,1,0:T(8,128)S(1)}, f32[16,8,128]{2,1,0:T(8,128)S(1)}, u32[]{:S(2)}, u32[]{:S(2)}) collective-permute-start(f32[16,8,128]{2,1,0:T(8,128)S(1)} %get-tuple-element.23), channel_id=1, source_target_pairs={{0,1},{1,0},{2,3},{3,2},{4,5},{5,4},{6,7},{7,6},{8,9},{9,8},{10,11... | collective-permute-start | bytes 196616 | tf_op jit(solution)/shard_map/ppermute | solution.py:20
  17.9 8.9 %collective-permute-start.18 = (bf16[256,512]{1,0:T(8,128)(2,1)S(1)}, bf16[256,512]{1,0:T(8,128)(2,1)}, u32[]{:S(2)}, u32[]{:S(2)}) collective-permute-start(bf16[256,512]{1,0:T(8,128)(2,1)S(1)} %get-tuple-element.21.refs_14_.refs_10_), channel_id=1, source_target_pairs={{0,1},{1,0},{2,4},{3,5},{4,2},{5,3},{6,7},{7,6},{8,9},{9,8},{10,12... | collective-permute-start | bytes 786440 | tf_op jit(solution)/shard_map/ppermute | solution.py:20
  18.0 14.6 %collective-permute-start.17 = (bf16[256,512]{1,0:T(8,128)(2,1)S(1)}, bf16[256,512]{1,0:T(8,128)(2,1)S(1)}, u32[]{:S(2)}, u32[]{:S(2)}) collective-permute-start(bf16[256,512]{1,0:T(8,128)(2,1)S(1)} %get-tuple-element.21.refs_14_.refs_10_), channel_id=1, source_target_pairs={{0,2},{1,3},{2,0},{3,1},{4,6},{5,7},{6,4},{7,5},{8,10},{9,11},{10,... | collective-permute-start | bytes 786440 | tf_op jit(solution)/shard_map/ppermute | solution.py:20
  20.7 19.0 %collective-permute-start.13 = (bf16[256,512]{1,0:T(8,128)(2,1)S(1)}, bf16[256,512]{1,0:T(8,128)(2,1)S(1)}, u32[]{:S(2)}, u32[]{:S(2)}) collective-permute-start(bf16[256,512]{1,0:T(8,128)(2,1)S(1)} %get-tuple-element.22.refs_6_.refs_2_), channel_id=1, source_target_pairs={{0,1},{1,0},{2,3},{3,2},{4,5},{5,4},{6,7},{7,6},{8,9},{9,8},{10,11... | collective-permute-start | bytes 786440 | tf_op jit(solution)/shard_map/ppermute | solution.py:20
  20.7 19.6 %collective-permute-start.10 = (bf16[256,512]{1,0:T(8,128)(2,1)S(1)}, bf16[256,512]{1,0:T(8,128)(2,1)}, u32[]{:S(2)}, u32[]{:S(2)}) collective-permute-start(bf16[256,512]{1,0:T(8,128)(2,1)S(1)} %collective-permute-done.9), channel_id=1, source_target_pairs={{0,2},{1,3},{2,0},{3,1},{4,6},{5,7},{6,4},{7,5},{8,10},{9,11},{10,... | collective-permute-start | bytes 786440 | tf_op jit(solution)/shard_map/ppermute | solution.py:20
  26.8 15.0 %collective-permute-start.11 = (bf16[256,512]{1,0:T(8,128)(2,1)S(1)}, bf16[256,512]{1,0:T(8,128)(2,1)}, u32[]{:S(2)}, u32[]{:S(2)}) collective-permute-start(bf16[256,512]{1,0:T(8,128)(2,1)S(1)} %collective-permute-done.8.refs_7_.refs_3_), channel_id=1, source_target_pairs={{0,1},{1,0},{2,4},{3,5},{4,2},{5,3},{6,7},{7,6},{8,9},{9,8},{10,12... | collective-permute-start | bytes 786440 | tf_op jit(solution)/shard_map/ppermute | solution.py:20
  26.8 16.1 %collective-permute-start.19 = (bf16[256,512]{1,0:T(8,128)(2,1)}, bf16[256,512]{1,0:T(8,128)(2,1)}, u32[]{:S(2)}, u32[]{:S(2)}) collective-permute-start(bf16[256,512]{1,0:T(8,128)(2,1)} %collective-permute-done.18), channel_id=1, source_target_pairs={{0,2},{1,3},{2,0},{3,1},{4,6},{5,7},{6,4},{7,5},{8,10},{9,11},{10,... | collective-permute-start | bytes 786440 | tf_op jit(solution)/shard_map/ppermute | solution.py:20
  32.5 11.0 %collective-permute-start.20 = (bf16[256,512]{1,0:T(8,128)(2,1)S(1)}, bf16[256,512]{1,0:T(8,128)(2,1)}, u32[]{:S(2)}, u32[]{:S(2)}) collective-permute-start(bf16[256,512]{1,0:T(8,128)(2,1)S(1)} %collective-permute-done.17.refs_15_.refs_11_), channel_id=1, source_target_pairs={{0,1},{1,0},{2,4},{3,5},{4,2},{5,3},{6,7},{7,6},{8,9},{9,8},{10,12... | collective-permute-start | bytes 786440 | tf_op jit(solution)/shard_map/ppermute | solution.py:20
  39.7 5.7 %collective-permute-start.22 = (bf16[256,512]{1,0:T(8,128)(2,1)S(1)}, bf16[256,512]{1,0:T(8,128)(2,1)S(1)}, u32[]{:S(2)}, u32[]{:S(2)}) collective-permute-start(bf16[256,512]{1,0:T(8,128)(2,1)S(1)} %get-tuple-element.21.refs_14_.refs_10_), channel_id=1, source_target_pairs={{0,1},{1,0},{2,3},{3,2},{4,5},{5,4},{6,7},{7,6},{8,9},{9,8},{10,11... | collective-permute-start | bytes 786440 | tf_op jit(solution)/shard_map/ppermute | solution.py:20
  40.3 9.2 %collective-permute-start.4 = (bf16[64,2048]{1,0:T(8,128)(2,1)S(1)}, bf16[64,2048]{1,0:T(8,128)(2,1)S(1)}, u32[]{:S(2)}, u32[]{:S(2)}) collective-permute-start(bf16[64,2048]{1,0:T(8,128)(2,1)S(1)} %get-tuple-element.16.refs_0_), channel_id=1, source_target_pairs={{0,8},{8,0},{16,24},{24,16},{1,9},{9,1},{17,25},{25,17},{2,10},{10... | collective-permute-start | bytes 786440 | tf_op jit(solution)/shard_map/ppermute | solution.py:20
  41.8 9.9 %collective-permute-start.12 = (bf16[256,512]{1,0:T(8,128)(2,1)}, bf16[256,512]{1,0:T(8,128)(2,1)S(1)}, u32[]{:S(2)}, u32[]{:S(2)}) collective-permute-start(bf16[256,512]{1,0:T(8,128)(2,1)} %collective-permute-done.11), channel_id=1, source_target_pairs={{0,2},{1,3},{2,0},{3,1},{4,6},{5,7},{6,4},{7,5},{8,10},{9,11},{10,... | collective-permute-start | bytes 786440 | tf_op jit(solution)/shard_map/ppermute | solution.py:20
  43.0 11.3 %collective-permute-start.5 = (bf16[64,2048]{1,0:T(8,128)(2,1)S(1)}, bf16[64,2048]{1,0:T(8,128)(2,1)}, u32[]{:S(2)}, u32[]{:S(2)}) collective-permute-start(bf16[64,2048]{1,0:T(8,128)(2,1)S(1)} %get-tuple-element.17.refs_1_), channel_id=1, source_target_pairs={{0,8},{8,0},{16,24},{24,16},{1,9},{9,1},{17,25},{25,17},{2,10},{10... | collective-permute-start | bytes 786440 | tf_op jit(solution)/shard_map/ppermute | solution.py:20
  43.6 12.0 %collective-permute-start.21 = (bf16[256,512]{1,0:T(8,128)(2,1)}, bf16[256,512]{1,0:T(8,128)(2,1)S(1)}, u32[]{:S(2)}, u32[]{:S(2)}) collective-permute-start(bf16[256,512]{1,0:T(8,128)(2,1)} %collective-permute-done.20), channel_id=1, source_target_pairs={{0,2},{1,3},{2,0},{3,1},{4,6},{5,7},{6,4},{7,5},{8,10},{9,11},{10,... | collective-permute-start | bytes 786440 | tf_op jit(solution)/shard_map/ppermute | solution.py:20
  45.5 10.2 %collective-permute-start.6 = (bf16[64,2048]{1,0:T(8,128)(2,1)S(1)}, bf16[64,2048]{1,0:T(8,128)(2,1)}, u32[]{:S(2)}, u32[]{:S(2)}) collective-permute-start(bf16[64,2048]{1,0:T(8,128)(2,1)S(1)} %get-tuple-element.16.refs_0_), channel_id=1, source_target_pairs={{0,16},{8,24},{16,0},{24,8},{1,17},{9,25},{17,1},{25,9},{2,18},{10... | collective-permute-start | bytes 786440 | tf_op jit(solution)/shard_map/ppermute | solution.py:20
  50.2 8.2 %collective-permute-start.7 = (bf16[64,2048]{1,0:T(8,128)(2,1)S(1)}, bf16[64,2048]{1,0:T(8,128)(2,1)S(1)}, u32[]{:S(2)}, u32[]{:S(2)}) collective-permute-start(bf16[64,2048]{1,0:T(8,128)(2,1)S(1)} %get-tuple-element.17.refs_1_), channel_id=1, source_target_pairs={{0,16},{8,24},{16,0},{24,8},{1,17},{9,25},{17,1},{25,9},{2,18},{10... | collective-permute-start | bytes 786440 | tf_op jit(solution)/shard_map/ppermute | solution.py:20
  51.7 7.3 %collective-permute-start.14 = (bf16[256,512]{1,0:T(8,128)(2,1)S(1)}, bf16[256,512]{1,0:T(8,128)(2,1)S(1)}, u32[]{:S(2)}, u32[]{:S(2)}) collective-permute-start(bf16[256,512]{1,0:T(8,128)(2,1)S(1)} %collective-permute-done.8.refs_7_.refs_3_), channel_id=1, source_target_pairs={{0,1},{1,0},{2,3},{3,2},{4,5},{5,4},{6,7},{7,6},{8,9},{9,8},{10,11... | collective-permute-start | bytes 786440 | tf_op jit(solution)/shard_map/ppermute | solution.py:20
  54.3 5.2 %collective-permute-start.23 = (bf16[256,512]{1,0:T(8,128)(2,1)S(1)}, bf16[256,512]{1,0:T(8,128)(2,1)S(1)}, u32[]{:S(2)}, u32[]{:S(2)}) collective-permute-start(bf16[256,512]{1,0:T(8,128)(2,1)S(1)} %collective-permute-done.17.refs_15_.refs_11_), channel_id=1, source_target_pairs={{0,1},{1,0},{2,3},{3,2},{4,5},{5,4},{6,7},{7,6},{8,9},{9,8},{10,11... | collective-permute-start | bytes 786440 | tf_op jit(solution)/shard_map/ppermute | solution.py:20
  55.6 5.4 %collective-permute-start.15 = (bf16[256,512]{1,0:T(8,128)(2,1)S(1)}, bf16[256,512]{1,0:T(8,128)(2,1)S(1)}, u32[]{:S(2)}, u32[]{:S(2)}) collective-permute-start(bf16[256,512]{1,0:T(8,128)(2,1)S(1)} %broadcast_select_fusion.3.refs_8_.refs_4_), channel_id=1, source_target_pairs={{0,1},{1,0},{2,3},{3,2},{4,5},{5,4},{6,7},{7,6},{8,9},{9,8},{10,11... | collective-permute-start | bytes 786440 | tf_op jit(solution)/shard_map/ppermute | solution.py:20
  55.7 7.0 %collective-permute-start.24 = (bf16[256,512]{1,0:T(8,128)(2,1)S(1)}, bf16[256,512]{1,0:T(8,128)(2,1)}, u32[]{:S(2)}, u32[]{:S(2)}) collective-permute-start(bf16[256,512]{1,0:T(8,128)(2,1)S(1)} %broadcast_select_fusion.1.refs_16_.refs_12_), channel_id=1, source_target_pairs={{0,1},{1,0},{2,3},{3,2},{4,5},{5,4},{6,7},{7,6},{8,9},{9,8},{10,11... | collective-permute-start | bytes 786440 | tf_op jit(solution)/shard_map/ppermute | solution.py:20
  59.0 3.7 %collective-permute-start.16 = (bf16[256,512]{1,0:T(8,128)(2,1)S(1)}, bf16[256,512]{1,0:T(8,128)(2,1)}, u32[]{:S(2)}, u32[]{:S(2)}) collective-permute-start(bf16[256,512]{1,0:T(8,128)(2,1)S(1)} %broadcast_select_fusion.2.refs_9_.refs_5_), channel_id=1, source_target_pairs={{0,1},{1,0},{2,3},{3,2},{4,5},{5,4},{6,7},{7,6},{8,9},{9,8},{10,11... | collective-permute-start | bytes 786440 | tf_op jit(solution)/shard_map/ppermute | solution.py:20
  59.0 3.7 %collective-permute-start.25 = (bf16[256,512]{1,0:T(8,128)(2,1)S(1)}, bf16[256,512]{1,0:T(8,128)(2,1)}, u32[]{:S(2)}, u32[]{:S(2)}) collective-permute-start(bf16[256,512]{1,0:T(8,128)(2,1)S(1)} %broadcast_select_fusion.refs_17_.refs_13_), channel_id=1, source_target_pairs={{0,1},{1,0},{2,3},{3,2},{4,5},{5,4},{6,7},{7,6},{8,9},{9,8},{10,11... | collective-permute-start | bytes 786440 | tf_op jit(solution)/shard_map/ppermute | solution.py:20
  59.5 12.4 %collective-permute-start.28 = (bf16[64,2048]{1,0:T(8,128)(2,1)}, bf16[64,2048]{1,0:T(8,128)(2,1)}, u32[]{:S(2)}, u32[]{:S(2)}) collective-permute-start(bf16[64,2048]{1,0:T(8,128)(2,1)} %collective-permute-done.6.refs_4_), channel_id=1, source_target_pairs={{0,8},{8,0},{16,24},{24,16},{1,9},{9,1},{17,25},{25,17},{2,10},{10... | collective-permute-start | bytes 786440 | tf_op jit(solution)/shard_map/ppermute | solution.py:20
  61.0 10.9 %collective-permute-start.29 = (bf16[64,2048]{1,0:T(8,128)(2,1)}, bf16[64,2048]{1,0:T(8,128)(2,1)}, u32[]{:S(2)}, u32[]{:S(2)}) collective-permute-start(bf16[64,2048]{1,0:T(8,128)(2,1)} %collective-permute-done.5.refs_3_), channel_id=1, source_target_pairs={{0,16},{8,24},{16,0},{24,8},{1,17},{9,25},{17,1},{25,9},{2,18},{10... | collective-permute-start | bytes 786440 | tf_op jit(solution)/shard_map/ppermute | solution.py:20
  70.6 9.0 %collective-permute-start.26 = (bf16[128,1024]{1,0:T(8,128)(2,1)S(1)}, bf16[128,1024]{1,0:T(8,128)(2,1)S(1)}, u32[]{:S(2)}, u32[]{:S(2)}) collective-permute-start(bf16[128,1024]{1,0:T(8,128)(2,1)S(1)} %get-tuple-element.19), channel_id=1, source_target_pairs={{0,8},{8,0},{16,24},{24,16},{1,9},{9,1},{17,25},{25,17},{2,10},{10... | collective-permute-start | bytes 786440 | tf_op jit(solution)/shard_map/ppermute | solution.py:20
  71.2 13.1 %collective-permute-start.27 = (bf16[128,1024]{1,0:T(8,128)(2,1)S(1)}, bf16[128,1024]{1,0:T(8,128)(2,1)S(1)}, u32[]{:S(2)}, u32[]{:S(2)}) collective-permute-start(bf16[128,1024]{1,0:T(8,128)(2,1)S(1)} %get-tuple-element.20), channel_id=1, source_target_pairs={{0,16},{8,24},{16,0},{24,8},{1,17},{9,25},{17,1},{25,9},{2,18},{10... | collective-permute-start | bytes 786440 | tf_op jit(solution)/shard_map/ppermute | solution.py:20
  74.9 10.9 %collective-permute-start.30 = (bf16[128,1024]{1,0:T(8,128)(2,1)S(1)}, bf16[128,1024]{1,0:T(8,128)(2,1)S(1)}, u32[]{:S(2)}, u32[]{:S(2)}) collective-permute-start(bf16[128,1024]{1,0:T(8,128)(2,1)S(1)} %shard_map.78), channel_id=1, source_target_pairs={{0,24},{8,16},{16,8},{24,0},{1,25},{9,17},{17,9},{25,1},{2,26},{10... | collective-permute-start | bytes 786440 | tf_op jit(solution)/shard_map/ppermute | solution.py:20
  (13 other events, 136.6 us)
where the time goes:
time: 87.7 us; the launch traced here: 87.2 us
  starting transfers between devices  37.9 us (43%)
  waiting for transfers between devices  18.2 us (21%)
  Pallas kernels  17.7 us (20%)
  local copies, waits for them, and re-layouts  10.9 us (12%)
  other arithmetic  2.15 us (2%)
    ppermute x31, starting transfers between devices, permute(): return lax.ppermute(array, axis, [(i, target(i)) for i in range(size)])  37.9 us
    ppermute x31, waiting for transfers between devices, permute(): return lax.ppermute(array, axis, [(i, target(i)) for i in range(size)])  18.2 us
    pallas_call x7, Pallas kernels, call(): pl.pallas_call(kernel, out_shape=out_shapes, in_specs=whole(scalars, pltp...  17.7 us
    unnamed x30, local copies, waits for them, and re-layouts  9.17 us
    select_n x2, other arithmetic, gather_rows(): second = jnp.where(inner, across, near_next)  1.98 us
  transfers between devices with their start and end apart: 31, of which 8 were waited for; matrix products, arithmetic and copies ran while one was open for 6% of the time, Pallas kernels for 17%

commit v1 on v0

v1 whole, which is shorter than its diff:
```python
import functools
import math

import jax
import jax.numpy as jnp
from jax import lax
from jax.experimental import pallas as pl
from jax.experimental.pallas import tpu as pltpu
from jax.sharding import PartitionSpec as P


F32 = jnp.float32
BF16 = jnp.bfloat16
LANES = 128
SUBLANES = 8


def permute(array, axis, target):
    size = lax.axis_size(axis)
    return lax.ppermute(array, axis, [(i, target(i)) for i in range(size)])


def swap(array, axis, mask):
    return permute(array, axis, lambda i: i ^ mask)


def position(axis):
    return lax.axis_index(axis).astype(jnp.int32)


def spread(ref, out_ref):
    order = ref.shape[0]
    for tile in range(ref.shape[1] // LANES):
        out_ref[tile * order : (tile + 1) * order, :] = ref[:, tile * LANES : (tile + 1) * LANES]


def modes_of(ref, first, order):
    return [ref[pl.ds(first * order + r, SUBLANES, stride=order), :] for r in range(order)]


def tree_sum(parts):
    while len(parts) > 1:
        parts = [parts[i] if i + 1 == len(parts) else parts[i] + parts[i + 1] for i in range(0, len(parts), 2)]
    return parts[0]


def group_of(slot, tiles):
    half = tiles // 2
    core = position("seq") & 1
    side = core if slot == 0 else 1 - core
    return pl.multiple_of(side * half, SUBLANES), half


def multiply(key_ref, value_ref, prod_ref):
    tokens, channels = key_ref.shape
    for tile in range(channels // LANES):
        cols = slice(tile * LANES, (tile + 1) * LANES)
        prod_ref[tile * tokens : (tile + 1) * tokens, :] = key_ref[:, cols].astype(F32) * value_ref[:, cols].astype(F32)


def slice_kernel(rows_ref, *refs):
    outs, sems = refs[:-1], refs[-1]
    columns = outs[0].shape[1]
    copies = []
    for i, out in enumerate(outs):
        start = pl.multiple_of((position("rep") * len(outs) + i) * columns, columns)
        copies.append(pltpu.make_async_copy(rows_ref.at[:, pl.ds(start, columns)], out, sems.at[i]))
    for copy in copies:
        copy.start()
    for copy in copies:
        copy.wait()


def state_kernel(*refs):
    fetched, (kept_ref, sent_ref, rate_ref) = refs[:3], refs[3:6]
    key_ref, value_ref, poles_ref, prod_ref, modes_ref, sems = refs[6:]
    copies = [
        pltpu.make_async_copy(source, held, sems.at[i])
        for i, (source, held) in enumerate(zip(fetched, (key_ref, value_ref, poles_ref)))
    ]
    for copy in copies:
        copy.start()
    for copy in copies:
        copy.wait()
    tokens, channels = key_ref.shape
    order, tiles = poles_ref.shape[0], channels // LANES
    spread(poles_ref, modes_ref)
    multiply(key_ref, value_ref, prod_ref)
    for slot, state_ref in ((1, sent_ref), (0, kept_ref)):
        start, half = group_of(slot, tiles)
        for row in range(0, half, SUBLANES):
            first = pl.multiple_of(start + row, SUBLANES)
            poles = modes_of(modes_ref, first, order)
            decay = [jnp.exp(-p) for p in poles]

            def step(t, state):
                x = prod_ref[pl.ds(first * tokens + t, SUBLANES, stride=tokens), :]
                return tuple(decay[r] * state[r] + x for r in range(order))

            zero = jnp.zeros((SUBLANES, LANES), F32)
            state = lax.fori_loop(0, tokens, step, (zero,) * order, unroll=8)
            for r in range(order):
                state_ref[r, row : row + SUBLANES, :] = state[r]
                if slot == 0:
                    rate_ref[r, row : row + SUBLANES, :] = jnp.exp(-poles[r] * float(tokens))


def local_kernel(key_ref, value_ref, poles_ref, residues_ref, skip_ref, local_ref, modes_ref, gains_ref, packed_ref):
    order, channels = poles_ref.shape
    tiles = channels // LANES
    tokens = key_ref.shape[0]
    spread(poles_ref, modes_ref)
    spread(residues_ref, gains_ref)
    multiply(key_ref, value_ref, local_ref)
    for first in range(0, tiles, SUBLANES):
        decay = [jnp.exp(-p) for p in modes_of(modes_ref, first, order)]
        for r, gain in enumerate(modes_of(gains_ref, first, order)):
            packed_ref[r] = gain
        skip = skip_ref[first : first + SUBLANES, :]

        def step(t, state):
            rows = pl.ds(first * tokens + t, SUBLANES, stride=tokens)
            x = local_ref[rows, :]
            state = tuple(decay[r] * state[r] + x for r in range(order))
            local_ref[rows, :] = tree_sum([packed_ref[r] * state[r] for r in range(order)] + [skip * x])
            return state

        zero = jnp.zeros((SUBLANES, LANES), F32)
        lax.fori_loop(0, tokens, step, (zero,) * order, unroll=4)


def carry_kernel(span, query_ref, local_ref, poles_ref, residues_ref, *refs):
    states, gated_refs = (refs[0:2], refs[2:4]), refs[4:-6]
    total_ref, starts_ref, modes_ref, gains_ref, held_ref, sem = refs[-6:]
    fetch = pltpu.make_async_copy(query_ref, held_ref, sem)
    fetch.start()
    tokens, channels = query_ref.shape
    order, tiles = poles_ref.shape[0], channels // LANES
    stretch = 16 if tokens % 16 == 0 else tokens
    spread(poles_ref, modes_ref)
    spread(residues_ref, gains_ref)
    shape = (SUBLANES, LANES)
    seq = position("seq")
    distance = jnp.full(shape, (seq & (span - 1)) * tokens, jnp.int32).astype(F32)
    counts = jnp.full(shape, (seq & span) != 0)
    for slot, (base_ref, arrived_ref) in enumerate(states):
        start, half = group_of(slot, tiles)
        for row in range(0, half, SUBLANES):
            first = pl.multiple_of(start + row, SUBLANES)
            poles = modes_of(modes_ref, first, order)
            jump = [jnp.exp(-p * float(stretch)) for p in poles]
            state = []
            for r in range(order):
                rows = slice(row, row + SUBLANES)
                reach = jnp.exp(-poles[r] * distance) * arrived_ref[r, rows, :]
                state.append(base_ref[r, rows, :] + jnp.where(counts, reach, 0.0))
            for i in range(tokens // stretch):
                for r in range(order):
                    starts_ref[i, r] = state[r]
                state = [jump[r] * state[r] for r in range(order)]
            decay = [jnp.exp(-p) for p in poles]

            def step(j, weight):
                weight = tuple(decay[r] * weight[r] for r in range(order))
                for i in range(tokens // stretch):
                    rows = pl.ds(first * tokens + i * stretch + j, SUBLANES, stride=tokens)
                    parts = [weight[r] * starts_ref[i, r] for r in range(order)] + [local_ref[rows, :]]
                    total_ref[rows, :] = tree_sum(parts)
                return weight

            lax.fori_loop(0, stretch, step, tuple(modes_of(gains_ref, first, order)))
    fetch.wait()
    step_rows = tokens // len(gated_refs)
    for tile in range(tiles):
        cols = slice(tile * LANES, (tile + 1) * LANES)
        y = total_ref[tile * tokens : (tile + 1) * tokens, :]
        gated = (held_ref[:, cols].astype(F32) * y).astype(BF16)
        for i, ref in enumerate(gated_refs):
            ref[:, cols] = gated[i * step_rows : (i + 1) * step_rows, :]


def project_kernel(pieces, places_of, chunks, earlier, *refs):
    places = places_of(position("seq"))
    blocks = len(places)
    gated, refs = refs[:pieces], refs[pieces:]
    weights, refs = refs[: blocks * chunks], refs[blocks * chunks :]
    before, outs = (refs[:chunks], refs[chunks:]) if earlier else (None, refs)
    depth, columns = weights[0].shape
    group = 2 if blocks % 2 == 0 else 1
    for n in range(chunks):
        total = before[n][...] if earlier else None
        for b in range(0, blocks, group):
            starts = [pl.multiple_of(places[b + i] * depth, depth) for i in range(group)]
            left = jnp.concatenate(
                [jnp.concatenate([g[:, pl.ds(s, depth)] for s in starts], axis=1) for g in gated], axis=0
            )
            right = jnp.concatenate([weights[n * blocks + b + i][...] for i in range(group)], axis=0)
            part = jnp.dot(left, right, preferred_element_type=F32)
            total = part if total is None else total + part
        if outs[0].dtype == F32:
            outs[n][...] = total
        else:
            rows = total.shape[0] // len(outs)
            for i, out in enumerate(outs):
                out[:, n * columns : (n + 1) * columns] = total[i * rows : (i + 1) * rows, :].astype(BF16)


def place_kernel(group, aliased, *refs):
    pieces, (out_ref, sems) = refs[int(aliased) : -2], refs[-2:]
    copies = []
    for i, piece in enumerate(pieces):
        width = piece.shape[1]
        start = pl.multiple_of((position("rep") ^ group[i]) * width, width)
        copies.append(pltpu.make_async_copy(piece, out_ref.at[:, pl.ds(start, width)], sems.at[i]))
    for copy in copies:
        copy.start()
    for copy in copies:
        copy.wait()


def call(kernel, out_shapes, args, scratch=(), flops=0, inputs=None, outputs=pltpu.VMEM, aliases=None):
    out_shapes = [jax.ShapeDtypeStruct(s, d) for s, d in out_shapes]
    inputs = inputs or [pltpu.VMEM] * len(args)
    size = lambda a: math.prod(a.shape) * jnp.dtype(a.dtype).itemsize
    held = sum(size(a) for a, space in zip(args, inputs) if space == pltpu.VMEM)
    held += sum(size(a) for a in out_shapes if outputs == pltpu.VMEM)
    held += sum(size(m) for m in scratch if getattr(m, "memory_space", None) == pltpu.VMEM)
    return pl.pallas_call(
        kernel,
        out_shape=out_shapes,
        in_specs=[pl.BlockSpec(memory_space=space) for space in inputs],
        out_specs=[pl.BlockSpec(memory_space=outputs)] * len(out_shapes),
        scratch_shapes=list(scratch),
        input_output_aliases=aliases or {},
        compiler_params=pltpu.CompilerParams(vmem_limit_bytes=min(2 * held + (2 << 20), 60 << 20)),
        cost_estimate=pl.CostEstimate(
            flops=flops, bytes_accessed=sum(size(a) for a in list(args) + out_shapes), transcendentals=0
        ),
    )(*args)


def fused(function, args, count):
    def kernel(*refs):
        for i in range(refs[0].shape[0]):
            results = function(*[ref[i] for ref in refs[: len(args)]])
            for ref, result in zip(refs[len(args) :], results):
                ref[i] = result

    return call(kernel, [(args[0].shape, args[0].dtype)] * count, args)


def carry_in(kept, sent, rate, members):
    def bit(span):
        return (position("seq") & span) != 0

    other = swap(sent, "seq", 1)

    def pair(rate, kept, other):
        later = bit(1)
        return (rate * jnp.where(later, other, kept) + jnp.where(later, kept, other),)

    (total,) = fused(pair, (rate, kept, other), 1)
    span = 2
    carried = ()
    while span * 2 < members:
        arrived = swap(total, "seq", span)

        def join(rate, total, arrived, *carried, span=span):
            prefix, ahead = carried or (jnp.zeros_like(rate), jnp.ones_like(rate))
            step = rate
            for _ in range(span.bit_length() - 1):
                step = step * step
            upper = bit(span)
            prefix = prefix + jnp.where(upper, ahead * arrived, 0.0)
            ahead = jnp.where(upper, ahead * step, ahead)
            total = step * jnp.where(upper, arrived, total) + jnp.where(upper, total, arrived)
            return total, prefix, ahead

        total, *carried = fused(join, (rate, total, arrived, *carried), 3)
        span *= 2
    arrived = swap(total, "seq", span)

    def bases(rate, kept, other, prefix):
        second = bit(1)
        early = jnp.where(second, other, kept)
        later = rate * prefix + early
        return jnp.where(second, later, prefix), jnp.where(second, prefix, later)

    own, away = fused(bases, (rate, kept, other, carried[0]), 2)
    rest = swap(away, "seq", 1)
    return own, arrived, rest, swap(arrived, "seq", 1), span


def gather_rows(block, members):
    if members != 8:
        rows = lax.all_gather(block, "seq", axis=0, tiled=True)
        return [rows], lambda seq: [0]

    def inner(seq):
        spot = seq >> 1
        return (spot == 1) | (spot == 2)

    def choose(first, second):
        def kernel(first_ref, second_ref, out_ref):
            @pl.when(inner(position("seq")))
            def _():
                out_ref[...] = first_ref[...]

            @pl.when(jnp.logical_not(inner(position("seq"))))
            def _():
                out_ref[...] = second_ref[...]

        return call(kernel, [(first.shape, first.dtype)], (first, second))[0]

    def middle(i):
        return {2: 4, 3: 5, 4: 2, 5: 3}.get(i, i ^ 1)

    near = swap(block, "seq", 2)
    across = permute(block, "seq", middle)
    near_next = swap(across, "seq", 2)
    across_next = permute(near, "seq", middle)
    far = swap(across_next, "seq", 2)
    second = choose(across, near_next)
    third = choose(across_next, far)
    mine = [block, near, second, third]
    theirs = [swap(b, "seq", 1) for b in mine]

    def places(seq):
        spot, core = seq >> 1, seq & 1
        opposite, skipped = 3 - spot, spot ^ 2
        spots = [
            spot,
            spot ^ 1,
            jnp.where(inner(seq), opposite, skipped),
            jnp.where(inner(seq), skipped, opposite),
        ]
        return sum(([p * 2 + core, p * 2 + 1 - core] for p in spots), [])

    return sum(([m, t] for m, t in zip(mine, theirs)), []), places


def gather_parts(halves, parts):
    if parts != 4 or len(halves) != 2:
        return [halves] + [[swap(h, "rep", i) for h in halves] for i in range(1, parts)]
    one = [swap(h, "rep", 1) for h in halves]
    two = [swap(h, "rep", 2) for h in halves]
    three = [swap(two[0], "rep", 1), swap(one[1], "rep", 2)]
    return [halves, one, two, three]


def shards(chunks, query, key_proj, value, poles, residues, skip, w_out):
    tokens, channels = query.shape
    width = w_out.shape[1]
    members = lax.axis_size("seq")
    parts = lax.axis_size("rep")
    order = poles.shape[1]
    tiles = channels // LANES
    part_width = width // parts
    columns = part_width // chunks
    remote = pltpu.HBM

    sliced = call(
        slice_kernel,
        [((w_out.shape[0], columns), BF16)] * chunks,
        (w_out,),
        [pltpu.SemaphoreType.DMA((chunks,))],
        inputs=[remote],
    )
    weights = []
    for n in range(chunks):
        rows, places = gather_rows(sliced[n], members)
        weights.append(rows)

    poles = poles.T
    residues = residues.T
    skip = skip.reshape(tiles, LANES)
    sums = ((tiles * tokens, LANES), F32)
    modes = pltpu.VMEM((tiles * order, LANES), F32)
    work = tokens * channels * order
    kept, sent, rate = call(
        state_kernel,
        [((order, tiles // 2, LANES), F32)] * 3,
        (key_proj, value, poles),
        [
            pltpu.VMEM((tokens, channels), BF16),
            pltpu.VMEM((tokens, channels), BF16),
            pltpu.VMEM((order, channels), F32),
            pltpu.VMEM(*sums),
            modes,
            pltpu.SemaphoreType.DMA((3,)),
        ],
        flops=2 * work,
        inputs=[remote] * 3,
    )
    own, arrived, rest, rest_arrived, span = carry_in(kept, sent, rate, members)
    (local,) = call(
        local_kernel,
        [sums],
        (key_proj, value, poles, residues, skip),
        [modes, modes, pltpu.VMEM((order, SUBLANES, LANES), F32)],
        flops=4 * work,
    )
    halves = call(
        functools.partial(carry_kernel, span),
        [((tokens // 2, channels), BF16)] * 2,
        (query, local, poles, residues, own, arrived, rest, rest_arrived),
        [
            pltpu.VMEM(*sums),
            pltpu.VMEM((tokens // 16, order, SUBLANES, LANES), F32),
            modes,
            modes,
            pltpu.VMEM((tokens, channels), BF16),
            pltpu.SemaphoreType.DMA,
        ],
        flops=2 * work,
        inputs=[remote] + [pltpu.VMEM] * 7,
    )
    gathered = gather_parts(list(halves), parts)

    def project(group, first, last, earlier=None, final=True):
        held = sum(group, [])
        rows = sum(h.shape[0] for h in held)
        chosen = sum((w[first:last] for w in weights), [])
        shapes = [((tokens, part_width), BF16)] * len(group) if final else [((rows, columns), F32)] * chunks
        return call(
            functools.partial(
                project_kernel, len(held), lambda seq: places(seq)[first:last], chunks, earlier is not None
            ),
            shapes,
            (*held, *chosen, *(earlier or ())),
            flops=2 * rows * chosen[0].shape[0] * len(chosen) * columns,
        )

    count = len(weights[0])
    split = max(count - 2, 0)
    if split > 0:
        partial = project(gathered[:-1], 0, split, final=False)
        blocks = project(gathered[:-1], split, count, earlier=partial)
    else:
        blocks = project(gathered[:-1], 0, count)
    blocks = list(blocks) + list(project(gathered[-1:], 0, count))
    pieces = [blocks[0]] + [swap(blocks[i], "rep", i) for i in range(1, parts)]
    mixed = None
    for group in (range(parts // 2), range(parts // 2, parts)):
        first = mixed is None
        (mixed,) = call(
            functools.partial(place_kernel, group, not first),
            [((tokens, width), BF16)],
            ([] if first else [mixed]) + [pieces[i] for i in group],
            [pltpu.SemaphoreType.DMA((len(group),))],
            inputs=([] if first else [remote]) + [pltpu.VMEM] * len(group),
            outputs=remote,
            aliases=None if first else {0: 0},
        )
    return mixed


def solution(mesh):
    chunks = 2

    def body(*args):
        return shards(chunks, *args)

    return jax.shard_map(
        body,
        mesh=mesh,
        in_specs=(
            P(("rep", "seq"), None),
            P(("rep", "seq"), None),
            P(("rep", "seq"), None),
            P(),
            P(),
            P(),
            P("seq", None),
        ),
        out_specs=P(("rep", "seq"), None),
        check_vma=False,
    )
```

time: 87.7 us -> 88.5 us (level)
  waiting for transfers between devices: 18.2 us -> 44.8 us
  starting transfers between devices: 37.9 us -> 25.3 us
  local copies, waits for them, and re-layouts: 10.9 us -> 4.59 us
  Pallas kernels: 17.7 us -> 13.3 us
  other arithmetic: 2.15 us -> 0 us
    ppermute x31 -> x32, waiting for transfers between devices: 18.2 us -> 44.8 us  [permute(): return lax.ppermute(array, axis, [(i, target(i)) for i in range(size)])]
    ppermute x31 -> x32, starting transfers between devices: 37.9 us -> 25.3 us  [permute(): return lax.ppermute(array, axis, [(i, target(i)) for i in range(size)])]
    unnamed x30 -> x18, local copies, waits for them, and re-layouts: 9.17 us -> 4.59 us
    pallas_call x7 -> x16, Pallas kernels: 17.7 us -> 13.3 us  [call(): pl.pallas_call(kernel, out_shape=out_shapes, in_specs=[pl.BlockSpec(memor...]
    select_n x5 -> x0, other arithmetic: 2.12 us -> none  [the longest x2 1.98 us: gather_rows(): second = jnp.where(inner, across, near_next)]
    dynamic_slice x1 -> x0, local copies, waits for them, and re-layouts: 1.07 us -> none  [shards(): lax.dynamic_slice_in_dim(w_out, (rep * chunks + n) * columns, columns, 1)]
  transfers between devices with their start and end apart: 31 -> 32, of which waited for: 8 -> 13; matrix products, arithmetic and copies ran while one was open for 6% -> 0% of each run, Pallas kernels for 17% -> 11%
where the time goes in v1:
time: 88.5 us; the launch traced here: 88.2 us
  waiting for transfers between devices  44.8 us (51%)
  starting transfers between devices  25.3 us (29%)
  Pallas kernels  13.3 us (15%)
  local copies, waits for them, and re-layouts  4.59 us (5%)
    ppermute x32, waiting for transfers between devices, permute(): return lax.ppermute(array, axis, [(i, target(i)) for i in range(size)])  44.8 us
    ppermute x32, starting transfers between devices, permute(): return lax.ppermute(array, axis, [(i, target(i)) for i in range(size)])  25.3 us
    pallas_call x16, Pallas kernels, call(): pl.pallas_call(kernel, out_shape=out_shapes, in_specs=[pl.BlockSpec(memor...  13.3 us
    unnamed x18, local copies, waits for them, and re-layouts  4.59 us
  transfers between devices with their start and end apart: 32, of which 13 were waited for; matrix products, arithmetic and copies ran while one was open for 0% of the time, Pallas kernels for 11%

profile of v1, /device:TPU:0, one launch (start us, length us, event | category | flops | bytes accessed | tf_op | source)
XLA Modules:
  0.0 88.2 jit_solution(9480827173114688171)
XLA Ops:
  0.0 1.0 %copy-done.1 = bf16[128,2048]{1,0:T(8,128)(2,1)S(1)} copy-done((bf16[128,2048]{1,0:T(8,128)(2,1)S(1)}, bf16[128,2048]{1,0:T(8,128)(2,1)}, u32[]{:S(2)}) %copy-start.1) | copy-done | bytes 524312
  1.0 1.0 %copy-done.3 = bf16[128,2048]{1,0:T(8,128)(2,1)S(1)} copy-done((bf16[128,2048]{1,0:T(8,128)(2,1)S(1)}, bf16[128,2048]{1,0:T(8,128)(2,1)}, u32[]{:S(2)}) %copy-start.3) | copy-done | bytes 524312
  2.1 0.9 %copy-done.4 = f32[2048,16]{0,1:T(8,128)S(1)} copy-done((f32[2048,16]{0,1:T(8,128)S(1)}, f32[2048,16]{0,1:T(8,128)}, u32[]{:S(2)}) %copy-start.4) | copy-done | bytes 131096
  3.0 2.0 %shard_map.74 = (f32[16,8,128]{2,1,0:T(8,128)S(1)}, f32[16,8,128]{2,1,0:T(8,128)S(1)}, f32[16,8,128]{2,1,0:T(8,128)S(1)}) custom-call(bf16[128,2048]{1,0:T(8,128)(2,1)S(1)} %copy-done.1, bf16[128,2048]{1,0:T(8,128)(2,1)S(1)} %copy-done.3, f32[16,2048]{1,0:T(8,128)S(1)} %bitcast.3), custom_call_target="tpu_custom_call" | custom-call | flops 8388608 | bytes 1376256 | tf_op jit(solution)/shard_map/pallas_call | solution.py:228
  5.6 0.9 %collective-permute-done.refs_2_ = f32[16,8,128]{2,1,0:T(8,128)S(1)} collective-permute-done((f32[16,8,128]{2,1,0:T(8,128)S(1)}, f32[16,8,128]{2,1,0:T(8,128)S(1)}, u32[]{:S(2)}, u32[]{:S(2)}) %collective-permute-start) | collective-permute-done | bytes 65568 | tf_op jit(solution)/shard_map/ppermute | solution.py:20
  6.5 3.0 %collective-permute-start.1 = (f32[16,8,128]{2,1,0:T(8,128)S(1)}, f32[16,8,128]{2,1,0:T(8,128)S(1)}, u32[]{:S(2)}, u32[]{:S(2)}) collective-permute-start(f32[16,8,128]{2,1,0:T(8,128)S(1)} %shard_map.75.refs_1_), channel_id=1, source_target_pairs={{0,2},{1,3},{2,0},{3,1},{4,6},{5,7},{6,4},{7,5},{8,10},{9,11},{10,... | collective-permute-start | bytes 196616 | tf_op jit(solution)/shard_map/ppermute | solution.py:20
  9.5 2.4 %collective-permute-done.1.refs_2_ = f32[16,8,128]{2,1,0:T(8,128)S(1)} collective-permute-done((f32[16,8,128]{2,1,0:T(8,128)S(1)}, f32[16,8,128]{2,1,0:T(8,128)S(1)}, u32[]{:S(2)}, u32[]{:S(2)}) %collective-permute-start.1) | collective-permute-done | bytes 65568 | tf_op jit(solution)/shard_map/ppermute | solution.py:20
  12.6 1.6 %copy-done = bf16[256,4096]{1,0:T(8,128)(2,1)S(1)} copy-done((bf16[256,4096]{1,0:T(8,128)(2,1)S(1)}, bf16[256,4096]{1,0:T(8,128)(2,1)}, u32[]{:S(2)}) %copy-start) | copy-done | bytes 2097176
  14.9 3.0 %collective-permute-start.2 = (f32[16,8,128]{2,1,0:T(8,128)S(1)}, f32[16,8,128]{2,1,0:T(8,128)S(1)}, u32[]{:S(2)}, u32[]{:S(2)}) collective-permute-start(f32[16,8,128]{2,1,0:T(8,128)S(1)} %get-tuple-element.26), channel_id=1, source_target_pairs={{0,4},{1,5},{2,6},{3,7},{4,0},{5,1},{6,2},{7,3},{8,12},{9,13},{10,... | collective-permute-start | bytes 196616 | tf_op jit(solution)/shard_map/ppermute | solution.py:20
  17.9 1.5 %collective-permute-start.9 = (bf16[256,512]{1,0:T(8,128)(2,1)S(1)}, bf16[256,512]{1,0:T(8,128)(2,1)S(1)}, u32[]{:S(2)}, u32[]{:S(2)}) collective-permute-start(bf16[256,512]{1,0:T(8,128)(2,1)S(1)} %get-tuple-element.30.refs_6_.refs_2_), channel_id=1, source_target_pairs={{0,2},{1,3},{2,0},{3,1},{4,6},{5,7},{6,4},{7,5},{8,10},{9,11},{10,... | collective-permute-start | bytes 786440 | tf_op jit(solution)/shard_map/ppermute | solution.py:20
  19.4 8.3 %collective-permute-done.2.refs_1_ = f32[16,8,128]{2,1,0:T(8,128)S(1)} collective-permute-done((f32[16,8,128]{2,1,0:T(8,128)S(1)}, f32[16,8,128]{2,1,0:T(8,128)S(1)}, u32[]{:S(2)}, u32[]{:S(2)}) %collective-permute-start.2) | collective-permute-done | bytes 65568 | tf_op jit(solution)/shard_map/ppermute | solution.py:20
  27.6 1.3 %collective-permute-done.4.refs_3_ = f32[16,8,128]{2,1,0:T(8,128)S(1)} collective-permute-done((f32[16,8,128]{2,1,0:T(8,128)S(1)}, f32[16,8,128]{2,1,0:T(8,128)S(1)}, u32[]{:S(2)}, u32[]{:S(2)}) %collective-permute-start.4) | collective-permute-done | bytes 65568 | tf_op jit(solution)/shard_map/ppermute | solution.py:20
  29.1 1.9 %collective-permute-start.20 = (bf16[256,512]{1,0:T(8,128)(2,1)S(1)}, bf16[256,512]{1,0:T(8,128)(2,1)S(1)}, u32[]{:S(2)}, u32[]{:S(2)}) collective-permute-start(bf16[256,512]{1,0:T(8,128)(2,1)S(1)} %collective-permute-done.19.first_ref), channel_id=1, source_target_pairs={{0,2},{1,3},{2,0},{3,1},{4,6},{5,7},{6,4},{7,5},{8,10},{9,11},{10,... | collective-permute-start | bytes 786440 | tf_op jit(solution)/shard_map/ppermute | solution.py:20
  31.5 6.6 %collective-permute-done.13.refs_14_.refs_12_ = bf16[256,512]{1,0:T(8,128)(2,1)S(1)} collective-permute-done((bf16[256,512]{1,0:T(8,128)(2,1)S(1)}, bf16[256,512]{1,0:T(8,128)(2,1)S(1)}, u32[]{:S(2)}, u32[]{:S(2)}) %collective-permute-start.13) | collective-permute-done | bytes 262176 | tf_op jit(solution)/shard_map/ppermute | solution.py:20
  38.1 1.6 %collective-permute-start.25 = (bf16[256,512]{1,0:T(8,128)(2,1)S(1)}, bf16[256,512]{1,0:T(8,128)(2,1)S(1)}, u32[]{:S(2)}, u32[]{:S(2)}) collective-permute-start(bf16[256,512]{1,0:T(8,128)(2,1)S(1)} %collective-permute-done.24.first_ref), channel_id=1, source_target_pairs={{0,2},{1,3},{2,0},{3,1},{4,6},{5,7},{6,4},{7,5},{8,10},{9,11},{10,... | collective-permute-start | bytes 786440 | tf_op jit(solution)/shard_map/ppermute | solution.py:20
  39.7 4.0 %collective-permute-done.20.second_ref = bf16[256,512]{1,0:T(8,128)(2,1)S(1)} collective-permute-done((bf16[256,512]{1,0:T(8,128)(2,1)S(1)}, bf16[256,512]{1,0:T(8,128)(2,1)S(1)}, u32[]{:S(2)}, u32[]{:S(2)}) %collective-permute-start.20) | collective-permute-done | bytes 262176 | tf_op jit(solution)/shard_map/ppermute | solution.py:20
  43.7 3.8 %shard_map.73.local_ref = f32[2048,128]{1,0:T(8,128)S(1)} custom-call(bf16[128,2048]{1,0:T(8,128)(2,1)S(1)} %copy-done.2, bf16[128,2048]{1,0:T(8,128)(2,1)S(1)} %copy-done.3, f32[16,2048]{1,0:T(8,128)S(1)} %bitcast.4, f32[16,2048]{1,0:T(8,128)S(1)} %bitcast.6, f32[16,128]{1,0:T(8,128)S(1)} %bitcast.8), custom_call_target="tpu_custom_call" | custom-call | flops 16777216 | bytes 2367488 | tf_op jit(solution)/shard_map/pallas_call | solution.py:228
  47.5 2.4 %shard_map.78 = (bf16[64,2048]{1,0:T(8,128)(2,1)S(1)}, bf16[64,2048]{1,0:T(8,128)(2,1)S(1)}) custom-call(bf16[128,2048]{1,0:T(8,128)(2,1)S(1)} %copy-done.7, f32[2048,128]{1,0:T(8,128)S(1)} %shard_map.73.local_ref, f32[16,2048]{1,0:T(8,128)S(1)} %bitcast.5, f32[16,2048]{1,0:T(8,128)S(1)} %bitcast.7, f32[16,8,128]{2,1,0:T(8,128)S(1)} %get-tuple-element.25.refs_0_, ...), custom_call_target="tpu_custom_call" | custom-call | flops 8388608 | bytes 2621440 | tf_op jit(solution)/shard_map/pallas_call | solution.py:228
  49.9 1.6 %collective-permute-start.7 = (bf16[64,2048]{1,0:T(8,128)(2,1)S(1)}, bf16[64,2048]{1,0:T(8,128)(2,1)S(1)}, u32[]{:S(2)}, u32[]{:S(2)}) collective-permute-start(bf16[64,2048]{1,0:T(8,128)(2,1)S(1)} %get-tuple-element.28.refs_0_), channel_id=1, source_target_pairs={{0,16},{8,24},{16,0},{24,8},{1,17},{9,25},{17,1},{25,9},{2,18},{10... | collective-permute-start | bytes 786440 | tf_op jit(solution)/shard_map/ppermute | solution.py:20
  51.5 2.0 %collective-permute-start.15 = (bf16[256,512]{1,0:T(8,128)(2,1)S(1)}, bf16[256,512]{1,0:T(8,128)(2,1)S(1)}, u32[]{:S(2)}, u32[]{:S(2)}) collective-permute-start(bf16[256,512]{1,0:T(8,128)(2,1)S(1)} %collective-permute-done.14.first_ref), channel_id=1, source_target_pairs={{0,2},{1,3},{2,0},{3,1},{4,6},{5,7},{6,4},{7,5},{8,10},{9,11},{10,... | collective-permute-start | bytes 786440 | tf_op jit(solution)/shard_map/ppermute | solution.py:20
  53.6 1.5 %collective-permute-start.5 = (bf16[64,2048]{1,0:T(8,128)(2,1)S(1)}, bf16[64,2048]{1,0:T(8,128)(2,1)S(1)}, u32[]{:S(2)}, u32[]{:S(2)}) collective-permute-start(bf16[64,2048]{1,0:T(8,128)(2,1)S(1)} %get-tuple-element.28.refs_0_), channel_id=1, source_target_pairs={{0,8},{8,0},{16,24},{24,16},{1,9},{9,1},{17,25},{25,17},{2,10},{10... | collective-permute-start | bytes 786440 | tf_op jit(solution)/shard_map/ppermute | solution.py:20
  55.6 3.6 %collective-permute-done.7.refs_4_ = bf16[64,2048]{1,0:T(8,128)(2,1)S(1)} collective-permute-done((bf16[64,2048]{1,0:T(8,128)(2,1)S(1)}, bf16[64,2048]{1,0:T(8,128)(2,1)S(1)}, u32[]{:S(2)}, u32[]{:S(2)}) %collective-permute-start.7) | collective-permute-done | bytes 262176 | tf_op jit(solution)/shard_map/ppermute | solution.py:20
  59.2 1.5 %collective-permute-start.6 = (bf16[64,2048]{1,0:T(8,128)(2,1)S(1)}, bf16[64,2048]{1,0:T(8,128)(2,1)S(1)}, u32[]{:S(2)}, u32[]{:S(2)}) collective-permute-start(bf16[64,2048]{1,0:T(8,128)(2,1)S(1)} %get-tuple-element.29.refs_1_), channel_id=1, source_target_pairs={{0,8},{8,0},{16,24},{24,16},{1,9},{9,1},{17,25},{25,17},{2,10},{10... | collective-permute-start | bytes 786440 | tf_op jit(solution)/shard_map/ppermute | solution.py:20
  60.7 4.8 %collective-permute-done.15.second_ref = bf16[256,512]{1,0:T(8,128)(2,1)S(1)} collective-permute-done((bf16[256,512]{1,0:T(8,128)(2,1)S(1)}, bf16[256,512]{1,0:T(8,128)(2,1)S(1)}, u32[]{:S(2)}, u32[]{:S(2)}) %collective-permute-start.15) | collective-permute-done | bytes 262176 | tf_op jit(solution)/shard_map/ppermute | solution.py:20
  67.0 1.5 %collective-permute-start.29 = (bf16[64,2048]{1,0:T(8,128)(2,1)S(1)}, bf16[64,2048]{1,0:T(8,128)(2,1)S(1)}, u32[]{:S(2)}, u32[]{:S(2)}) collective-permute-start(bf16[64,2048]{1,0:T(8,128)(2,1)S(1)} %collective-permute-done.7.refs_4_), channel_id=1, source_target_pairs={{0,8},{8,0},{16,24},{24,16},{1,9},{9,1},{17,25},{25,17},{2,10},{10... | collective-permute-start | bytes 786440 | tf_op jit(solution)/shard_map/ppermute | solution.py:20
  68.5 1.0 %collective-permute-start.30 = (bf16[64,2048]{1,0:T(8,128)(2,1)S(1)}, bf16[64,2048]{1,0:T(8,128)(2,1)S(1)}, u32[]{:S(2)}, u32[]{:S(2)}) collective-permute-start(bf16[64,2048]{1,0:T(8,128)(2,1)S(1)} %collective-permute-done.6.refs_3_), channel_id=1, source_target_pairs={{0,16},{8,24},{16,0},{24,8},{1,17},{9,25},{17,1},{25,9},{2,18},{10... | collective-permute-start | bytes 786440 | tf_op jit(solution)/shard_map/ppermute | solution.py:20
  69.6 1.4 %shard_map.84 = (f32[384,512]{1,0:T(8,128)S(1)}, f32[384,512]{1,0:T(8,128)S(1)}) custom-call(bf16[64,2048]{1,0:T(8,128)(2,1)S(1)} %get-tuple-element.28.refs_0_, bf16[64,2048]{1,0:T(8,128)(2,1)S(1)} %get-tuple-element.29.refs_1_, bf16[64,2048]{1,0:T(8,128)(2,1)S(1)} %collective-permute-done.5.refs_2_, bf16[64,2048]{1,0:T(8,128)(2,1)S(1)} %collective-permute-done.6.refs_3_, ...), custom_call_target="tpu_custom_call" | custom-call | flops 1207959552 | bytes 6291456 | tf_op jit(solution)/shard_map/pallas_call | solution.py:228
  72.2 1.0 %collective-permute-start.28 = (bf16[128,1024]{1,0:T(8,128)(2,1)S(1)}, bf16[128,1024]{1,0:T(8,128)(2,1)S(1)}, u32[]{:S(2)}, u32[]{:S(2)}) collective-permute-start(bf16[128,1024]{1,0:T(8,128)(2,1)S(1)} %get-tuple-element.36), channel_id=1, source_target_pairs={{0,16},{8,24},{16,0},{24,8},{1,17},{9,25},{17,1},{25,9},{2,18},{10... | collective-permute-start | bytes 786440 | tf_op jit(solution)/shard_map/ppermute | solution.py:20
  73.2 3.0 %collective-permute-done.29.refs_0_ = bf16[64,2048]{1,0:T(8,128)(2,1)S(1)} collective-permute-done((bf16[64,2048]{1,0:T(8,128)(2,1)S(1)}, bf16[64,2048]{1,0:T(8,128)(2,1)S(1)}, u32[]{:S(2)}, u32[]{:S(2)}) %collective-permute-start.29) | collective-permute-done | bytes 262176 | tf_op jit(solution)/shard_map/ppermute | solution.py:20
  76.2 1.5 %collective-permute-done.30.refs_1_ = bf16[64,2048]{1,0:T(8,128)(2,1)S(1)} collective-permute-done((bf16[64,2048]{1,0:T(8,128)(2,1)S(1)}, bf16[64,2048]{1,0:T(8,128)(2,1)S(1)}, u32[]{:S(2)}, u32[]{:S(2)}) %collective-permute-start.30) | collective-permute-done | bytes 262176 | tf_op jit(solution)/shard_map/ppermute | solution.py:20
  79.0 2.9 %collective-permute-done.27.refs_1_ = bf16[128,1024]{1,0:T(8,128)(2,1)S(1)} collective-permute-done((bf16[128,1024]{1,0:T(8,128)(2,1)S(1)}, bf16[128,1024]{1,0:T(8,128)(2,1)S(1)}, u32[]{:S(2)}, u32[]{:S(2)}) %collective-permute-start.27) | collective-permute-done | bytes 262176 | tf_op jit(solution)/shard_map/ppermute | solution.py:20
  82.6 4.7 %collective-permute-done.28.refs_1_ = bf16[128,1024]{1,0:T(8,128)(2,1)S(1)} collective-permute-done((bf16[128,1024]{1,0:T(8,128)(2,1)S(1)}, bf16[128,1024]{1,0:T(8,128)(2,1)S(1)}, u32[]{:S(2)}, u32[]{:S(2)}) %collective-permute-start.28) | collective-permute-done | bytes 262176 | tf_op jit(solution)/shard_map/ppermute | solution.py:20
  (66 shorter events, 8.8 us)
Async XLA Ops:
  5.0 1.5 %collective-permute-start = (f32[16,8,128]{2,1,0:T(8,128)S(1)}, f32[16,8,128]{2,1,0:T(8,128)S(1)}, u32[]{:S(2)}, u32[]{:S(2)}) collective-permute-start(f32[16,8,128]{2,1,0:T(8,128)S(1)} %get-tuple-element.23), channel_id=1, source_target_pairs={{0,1},{1,0},{2,3},{3,2},{4,5},{5,4},{6,7},{7,6},{8,9},{9,8},{10,11... | collective-permute-start | bytes 196616 | tf_op jit(solution)/shard_map/ppermute | solution.py:20
  6.5 5.4 %collective-permute-start.1 = (f32[16,8,128]{2,1,0:T(8,128)S(1)}, f32[16,8,128]{2,1,0:T(8,128)S(1)}, u32[]{:S(2)}, u32[]{:S(2)}) collective-permute-start(f32[16,8,128]{2,1,0:T(8,128)S(1)} %shard_map.75.refs_1_), channel_id=1, source_target_pairs={{0,2},{1,3},{2,0},{3,1},{4,6},{5,7},{6,4},{7,5},{8,10},{9,11},{10,... | collective-permute-start | bytes 196616 | tf_op jit(solution)/shard_map/ppermute | solution.py:20
  12.6 6.8 %collective-permute-start.3 = (f32[16,8,128]{2,1,0:T(8,128)S(1)}, f32[16,8,128]{2,1,0:T(8,128)S(1)}, u32[]{:S(2)}, u32[]{:S(2)}) collective-permute-start(f32[16,8,128]{2,1,0:T(8,128)S(1)} %get-tuple-element.27), channel_id=1, source_target_pairs={{0,1},{1,0},{2,3},{3,2},{4,5},{5,4},{6,7},{7,6},{8,9},{9,8},{10,11... | collective-permute-start | bytes 196616 | tf_op jit(solution)/shard_map/ppermute | solution.py:20
  14.3 14.6 %collective-permute-start.19 = (bf16[256,512]{1,0:T(8,128)(2,1)S(1)}, bf16[256,512]{1,0:T(8,128)(2,1)S(1)}, u32[]{:S(2)}, u32[]{:S(2)}) collective-permute-start(bf16[256,512]{1,0:T(8,128)(2,1)S(1)} %get-tuple-element.30.refs_6_.refs_2_), channel_id=1, source_target_pairs={{0,1},{1,0},{2,4},{3,5},{4,2},{5,3},{6,7},{7,6},{8,9},{9,8},{10,12... | collective-permute-start | bytes 786440 | tf_op jit(solution)/shard_map/ppermute | solution.py:20
  14.9 14.2 %collective-permute-start.17 = (bf16[256,512]{1,0:T(8,128)(2,1)S(1)}, bf16[256,512]{1,0:T(8,128)(2,1)S(1)}, u32[]{:S(2)}, u32[]{:S(2)}) collective-permute-start(bf16[256,512]{1,0:T(8,128)(2,1)S(1)} %get-tuple-element.30.refs_6_.refs_2_), channel_id=1, source_target_pairs={{0,1},{1,0},{2,3},{3,2},{4,5},{5,4},{6,7},{7,6},{8,9},{9,8},{10,11... | collective-permute-start | bytes 786440 | tf_op jit(solution)/shard_map/ppermute | solution.py:20
  14.9 12.7 %collective-permute-start.2 = (f32[16,8,128]{2,1,0:T(8,128)S(1)}, f32[16,8,128]{2,1,0:T(8,128)S(1)}, u32[]{:S(2)}, u32[]{:S(2)}) collective-permute-start(f32[16,8,128]{2,1,0:T(8,128)S(1)} %get-tuple-element.26), channel_id=1, source_target_pairs={{0,4},{1,5},{2,6},{3,7},{4,0},{5,1},{6,2},{7,3},{8,12},{9,13},{10,... | collective-permute-start | bytes 196616 | tf_op jit(solution)/shard_map/ppermute | solution.py:20
  17.9 13.1 %collective-permute-start.9 = (bf16[256,512]{1,0:T(8,128)(2,1)S(1)}, bf16[256,512]{1,0:T(8,128)(2,1)S(1)}, u32[]{:S(2)}, u32[]{:S(2)}) collective-permute-start(bf16[256,512]{1,0:T(8,128)(2,1)S(1)} %get-tuple-element.30.refs_6_.refs_2_), channel_id=1, source_target_pairs={{0,2},{1,3},{2,0},{3,1},{4,6},{5,7},{6,4},{7,5},{8,10},{9,11},{10,... | collective-permute-start | bytes 786440 | tf_op jit(solution)/shard_map/ppermute | solution.py:20
  19.4 11.8 %collective-permute-start.24 = (bf16[256,512]{1,0:T(8,128)(2,1)S(1)}, bf16[256,512]{1,0:T(8,128)(2,1)S(1)}, u32[]{:S(2)}, u32[]{:S(2)}) collective-permute-start(bf16[256,512]{1,0:T(8,128)(2,1)S(1)} %get-tuple-element.31.refs_12_.refs_10_), channel_id=1, source_target_pairs={{0,1},{1,0},{2,4},{3,5},{4,2},{5,3},{6,7},{7,6},{8,9},{9,8},{10,12... | collective-permute-start | bytes 786440 | tf_op jit(solution)/shard_map/ppermute | solution.py:20
  27.6 1.3 %collective-permute-start.4 = (f32[16,8,128]{2,1,0:T(8,128)S(1)}, f32[16,8,128]{2,1,0:T(8,128)S(1)}, u32[]{:S(2)}, u32[]{:S(2)}) collective-permute-start(f32[16,8,128]{2,1,0:T(8,128)S(1)} %collective-permute-done.2.refs_1_), channel_id=1, source_target_pairs={{0,1},{1,0},{2,3},{3,2},{4,5},{5,4},{6,7},{7,6},{8,9},{9,8},{10,11... | collective-permute-start | bytes 196616 | tf_op jit(solution)/shard_map/ppermute | solution.py:20
  28.9 9.2 %collective-permute-start.13 = (bf16[256,512]{1,0:T(8,128)(2,1)S(1)}, bf16[256,512]{1,0:T(8,128)(2,1)S(1)}, u32[]{:S(2)}, u32[]{:S(2)}) collective-permute-start(bf16[256,512]{1,0:T(8,128)(2,1)S(1)} %get-tuple-element.31.refs_12_.refs_10_), channel_id=1, source_target_pairs={{0,2},{1,3},{2,0},{3,1},{4,6},{5,7},{6,4},{7,5},{8,10},{9,11},{10,... | collective-permute-start | bytes 786440 | tf_op jit(solution)/shard_map/ppermute | solution.py:20
  28.9 9.2 %collective-permute-start.22 = (bf16[256,512]{1,0:T(8,128)(2,1)S(1)}, bf16[256,512]{1,0:T(8,128)(2,1)S(1)}, u32[]{:S(2)}, u32[]{:S(2)}) collective-permute-start(bf16[256,512]{1,0:T(8,128)(2,1)S(1)} %get-tuple-element.31.refs_12_.refs_10_), channel_id=1, source_target_pairs={{0,1},{1,0},{2,3},{3,2},{4,5},{5,4},{6,7},{7,6},{8,9},{9,8},{10,11... | collective-permute-start | bytes 786440 | tf_op jit(solution)/shard_map/ppermute | solution.py:20
  29.1 14.6 %collective-permute-start.20 = (bf16[256,512]{1,0:T(8,128)(2,1)S(1)}, bf16[256,512]{1,0:T(8,128)(2,1)S(1)}, u32[]{:S(2)}, u32[]{:S(2)}) collective-permute-start(bf16[256,512]{1,0:T(8,128)(2,1)S(1)} %collective-permute-done.19.first_ref), channel_id=1, source_target_pairs={{0,2},{1,3},{2,0},{3,1},{4,6},{5,7},{6,4},{7,5},{8,10},{9,11},{10,... | collective-permute-start | bytes 786440 | tf_op jit(solution)/shard_map/ppermute | solution.py:20
  31.0 18.9 %collective-permute-start.18 = (bf16[256,512]{1,0:T(8,128)(2,1)S(1)}, bf16[256,512]{1,0:T(8,128)(2,1)S(1)}, u32[]{:S(2)}, u32[]{:S(2)}) collective-permute-start(bf16[256,512]{1,0:T(8,128)(2,1)S(1)} %collective-permute-done.9.refs_8_.refs_4_), channel_id=1, source_target_pairs={{0,1},{1,0},{2,3},{3,2},{4,5},{5,4},{6,7},{7,6},{8,9},{9,8},{10,11... | collective-permute-start | bytes 786440 | tf_op jit(solution)/shard_map/ppermute | solution.py:20
  31.2 20.4 %collective-permute-start.10 = (bf16[256,512]{1,0:T(8,128)(2,1)S(1)}, bf16[256,512]{1,0:T(8,128)(2,1)S(1)}, u32[]{:S(2)}, u32[]{:S(2)}) collective-permute-start(bf16[256,512]{1,0:T(8,128)(2,1)S(1)} %collective-permute-done.9.refs_8_.refs_4_), channel_id=1, source_target_pairs={{0,1},{1,0},{2,4},{3,5},{4,2},{5,3},{6,7},{7,6},{8,9},{9,8},{10,12... | collective-permute-start | bytes 786440 | tf_op jit(solution)/shard_map/ppermute | solution.py:20
  38.1 13.5 %collective-permute-start.14 = (bf16[256,512]{1,0:T(8,128)(2,1)S(1)}, bf16[256,512]{1,0:T(8,128)(2,1)S(1)}, u32[]{:S(2)}, u32[]{:S(2)}) collective-permute-start(bf16[256,512]{1,0:T(8,128)(2,1)S(1)} %collective-permute-done.13.refs_14_.refs_12_), channel_id=1, source_target_pairs={{0,1},{1,0},{2,4},{3,5},{4,2},{5,3},{6,7},{7,6},{8,9},{9,8},{10,12... | collective-permute-start | bytes 786440 | tf_op jit(solution)/shard_map/ppermute | solution.py:20
  38.1 15.5 %collective-permute-start.25 = (bf16[256,512]{1,0:T(8,128)(2,1)S(1)}, bf16[256,512]{1,0:T(8,128)(2,1)S(1)}, u32[]{:S(2)}, u32[]{:S(2)}) collective-permute-start(bf16[256,512]{1,0:T(8,128)(2,1)S(1)} %collective-permute-done.24.first_ref), channel_id=1, source_target_pairs={{0,2},{1,3},{2,0},{3,1},{4,6},{5,7},{6,4},{7,5},{8,10},{9,11},{10,... | collective-permute-start | bytes 786440 | tf_op jit(solution)/shard_map/ppermute | solution.py:20
  43.7 11.4 %collective-permute-start.23 = (bf16[256,512]{1,0:T(8,128)(2,1)S(1)}, bf16[256,512]{1,0:T(8,128)(2,1)S(1)}, u32[]{:S(2)}, u32[]{:S(2)}) collective-permute-start(bf16[256,512]{1,0:T(8,128)(2,1)S(1)} %collective-permute-done.13.refs_14_.refs_12_), channel_id=1, source_target_pairs={{0,1},{1,0},{2,3},{3,2},{4,5},{5,4},{6,7},{7,6},{8,9},{9,8},{10,11... | collective-permute-start | bytes 786440 | tf_op jit(solution)/shard_map/ppermute | solution.py:20
  49.9 9.2 %collective-permute-start.7 = (bf16[64,2048]{1,0:T(8,128)(2,1)S(1)}, bf16[64,2048]{1,0:T(8,128)(2,1)S(1)}, u32[]{:S(2)}, u32[]{:S(2)}) collective-permute-start(bf16[64,2048]{1,0:T(8,128)(2,1)S(1)} %get-tuple-element.28.refs_0_), channel_id=1, source_target_pairs={{0,16},{8,24},{16,0},{24,8},{1,17},{9,25},{17,1},{25,9},{2,18},{10... | collective-permute-start | bytes 786440 | tf_op jit(solution)/shard_map/ppermute | solution.py:20
  51.5 9.2 %collective-permute-start.11 = (bf16[256,512]{1,0:T(8,128)(2,1)S(1)}, bf16[256,512]{1,0:T(8,128)(2,1)S(1)}, u32[]{:S(2)}, u32[]{:S(2)}) collective-permute-start(bf16[256,512]{1,0:T(8,128)(2,1)S(1)} %collective-permute-done.10.first_ref), channel_id=1, source_target_pairs={{0,2},{1,3},{2,0},{3,1},{4,6},{5,7},{6,4},{7,5},{8,10},{9,11},{10,... | collective-permute-start | bytes 786440 | tf_op jit(solution)/shard_map/ppermute | solution.py:20
  51.5 14.0 %collective-permute-start.15 = (bf16[256,512]{1,0:T(8,128)(2,1)S(1)}, bf16[256,512]{1,0:T(8,128)(2,1)S(1)}, u32[]{:S(2)}, u32[]{:S(2)}) collective-permute-start(bf16[256,512]{1,0:T(8,128)(2,1)S(1)} %collective-permute-done.14.first_ref), channel_id=1, source_target_pairs={{0,2},{1,3},{2,0},{3,1},{4,6},{5,7},{6,4},{7,5},{8,10},{9,11},{10,... | collective-permute-start | bytes 786440 | tf_op jit(solution)/shard_map/ppermute | solution.py:20
  53.6 12.1 %collective-permute-start.5 = (bf16[64,2048]{1,0:T(8,128)(2,1)S(1)}, bf16[64,2048]{1,0:T(8,128)(2,1)S(1)}, u32[]{:S(2)}, u32[]{:S(2)}) collective-permute-start(bf16[64,2048]{1,0:T(8,128)(2,1)S(1)} %get-tuple-element.28.refs_0_), channel_id=1, source_target_pairs={{0,8},{8,0},{16,24},{24,16},{1,9},{9,1},{17,25},{25,17},{2,10},{10... | collective-permute-start | bytes 786440 | tf_op jit(solution)/shard_map/ppermute | solution.py:20
  55.1 11.2 %collective-permute-start.8 = (bf16[64,2048]{1,0:T(8,128)(2,1)S(1)}, bf16[64,2048]{1,0:T(8,128)(2,1)S(1)}, u32[]{:S(2)}, u32[]{:S(2)}) collective-permute-start(bf16[64,2048]{1,0:T(8,128)(2,1)S(1)} %get-tuple-element.29.refs_1_), channel_id=1, source_target_pairs={{0,16},{8,24},{16,0},{24,8},{1,17},{9,25},{17,1},{25,9},{2,18},{10... | collective-permute-start | bytes 786440 | tf_op jit(solution)/shard_map/ppermute | solution.py:20
  59.2 7.9 %collective-permute-start.6 = (bf16[64,2048]{1,0:T(8,128)(2,1)S(1)}, bf16[64,2048]{1,0:T(8,128)(2,1)S(1)}, u32[]{:S(2)}, u32[]{:S(2)}) collective-permute-start(bf16[64,2048]{1,0:T(8,128)(2,1)S(1)} %get-tuple-element.29.refs_1_), channel_id=1, source_target_pairs={{0,8},{8,0},{16,24},{24,16},{1,9},{9,1},{17,25},{25,17},{2,10},{10... | collective-permute-start | bytes 786440 | tf_op jit(solution)/shard_map/ppermute | solution.py:20
  60.7 7.8 %collective-permute-start.21 = (bf16[256,512]{1,0:T(8,128)(2,1)S(1)}, bf16[256,512]{1,0:T(8,128)(2,1)S(1)}, u32[]{:S(2)}, u32[]{:S(2)}) collective-permute-start(bf16[256,512]{1,0:T(8,128)(2,1)S(1)} %shard_map.82.refs_10_.refs_6_), channel_id=1, source_target_pairs={{0,1},{1,0},{2,3},{3,2},{4,5},{5,4},{6,7},{7,6},{8,9},{9,8},{10,11... | collective-permute-start | bytes 786440 | tf_op jit(solution)/shard_map/ppermute | solution.py:20
  65.6 4.0 %collective-permute-start.26 = (bf16[256,512]{1,0:T(8,128)(2,1)S(1)}, bf16[256,512]{1,0:T(8,128)(2,1)S(1)}, u32[]{:S(2)}, u32[]{:S(2)}) collective-permute-start(bf16[256,512]{1,0:T(8,128)(2,1)S(1)} %shard_map.83.refs_16_.refs_14_), channel_id=1, source_target_pairs={{0,1},{1,0},{2,3},{3,2},{4,5},{5,4},{6,7},{7,6},{8,9},{9,8},{10,11... | collective-permute-start | bytes 786440 | tf_op jit(solution)/shard_map/ppermute | solution.py:20
  65.6 5.3 %collective-permute-start.12 = (bf16[256,512]{1,0:T(8,128)(2,1)S(1)}, bf16[256,512]{1,0:T(8,128)(2,1)S(1)}, u32[]{:S(2)}, u32[]{:S(2)}) collective-permute-start(bf16[256,512]{1,0:T(8,128)(2,1)S(1)} %shard_map.80.refs_6_.refs_8_), channel_id=1, source_target_pairs={{0,1},{1,0},{2,3},{3,2},{4,5},{5,4},{6,7},{7,6},{8,9},{9,8},{10,11... | collective-permute-start | bytes 786440 | tf_op jit(solution)/shard_map/ppermute | solution.py:20
  66.2 4.8 %collective-permute-start.16 = (bf16[256,512]{1,0:T(8,128)(2,1)S(1)}, bf16[256,512]{1,0:T(8,128)(2,1)S(1)}, u32[]{:S(2)}, u32[]{:S(2)}) collective-permute-start(bf16[256,512]{1,0:T(8,128)(2,1)S(1)} %shard_map.81.refs_8_.refs_16_), channel_id=1, source_target_pairs={{0,1},{1,0},{2,3},{3,2},{4,5},{5,4},{6,7},{7,6},{8,9},{9,8},{10,11... | collective-permute-start | bytes 786440 | tf_op jit(solution)/shard_map/ppermute | solution.py:20
  67.0 9.2 %collective-permute-start.29 = (bf16[64,2048]{1,0:T(8,128)(2,1)S(1)}, bf16[64,2048]{1,0:T(8,128)(2,1)S(1)}, u32[]{:S(2)}, u32[]{:S(2)}) collective-permute-start(bf16[64,2048]{1,0:T(8,128)(2,1)S(1)} %collective-permute-done.7.refs_4_), channel_id=1, source_target_pairs={{0,8},{8,0},{16,24},{24,16},{1,9},{9,1},{17,25},{25,17},{2,10},{10... | collective-permute-start | bytes 786440 | tf_op jit(solution)/shard_map/ppermute | solution.py:20
  68.5 9.2 %collective-permute-start.30 = (bf16[64,2048]{1,0:T(8,128)(2,1)S(1)}, bf16[64,2048]{1,0:T(8,128)(2,1)S(1)}, u32[]{:S(2)}, u32[]{:S(2)}) collective-permute-start(bf16[64,2048]{1,0:T(8,128)(2,1)S(1)} %collective-permute-done.6.refs_3_), channel_id=1, source_target_pairs={{0,16},{8,24},{16,0},{24,8},{1,17},{9,25},{17,1},{25,9},{2,18},{10... | collective-permute-start | bytes 786440 | tf_op jit(solution)/shard_map/ppermute | solution.py:20
  71.6 10.2 %collective-permute-start.27 = (bf16[128,1024]{1,0:T(8,128)(2,1)S(1)}, bf16[128,1024]{1,0:T(8,128)(2,1)S(1)}, u32[]{:S(2)}, u32[]{:S(2)}) collective-permute-start(bf16[128,1024]{1,0:T(8,128)(2,1)S(1)} %get-tuple-element.35), channel_id=1, source_target_pairs={{0,8},{8,0},{16,24},{24,16},{1,9},{9,1},{17,25},{25,17},{2,10},{10... | collective-permute-start | bytes 786440 | tf_op jit(solution)/shard_map/ppermute | solution.py:20
  72.2 15.2 %collective-permute-start.28 = (bf16[128,1024]{1,0:T(8,128)(2,1)S(1)}, bf16[128,1024]{1,0:T(8,128)(2,1)S(1)}, u32[]{:S(2)}, u32[]{:S(2)}) collective-permute-start(bf16[128,1024]{1,0:T(8,128)(2,1)S(1)} %get-tuple-element.36), channel_id=1, source_target_pairs={{0,16},{8,24},{16,0},{24,8},{1,17},{9,25},{17,1},{25,9},{2,18},{10... | collective-permute-start | bytes 786440 | tf_op jit(solution)/shard_map/ppermute | solution.py:20
  78.5 8.9 %collective-permute-start.31 = (bf16[128,1024]{1,0:T(8,128)(2,1)S(1)}, bf16[128,1024]{1,0:T(8,128)(2,1)S(1)}, u32[]{:S(2)}, u32[]{:S(2)}) collective-permute-start(bf16[128,1024]{1,0:T(8,128)(2,1)S(1)} %shard_map.87), channel_id=1, source_target_pairs={{0,24},{8,16},{16,8},{24,0},{1,25},{9,17},{17,9},{25,1},{2,26},{10... | collective-permute-start | bytes 786440 | tf_op jit(solution)/shard_map/ppermute | solution.py:20
  (9 other events, 193.3 us)
